TPU v7x, 512 devices: a whole 4x4x16 slice. The times are simulated.
512 devices in a mesh: mp: 4 (over z_hi), space: 128 (over y, z_lo, x, core).
Axes of the slice: x: 4, y: 4, z: 16 (z_hi: 4, z_lo: 4; z = z_hi * 4 + z_lo), core: 2. Of those that a mesh axis runs over, the one named last changes fastest.
Arguments:
- positions: float32 [3, 8192], P(None, 'space'), may hold values from 0 to 1
- send_lists: int32 [128, 6, 128], P('space'), may hold values from -1 to 575, as said below
- neighbours: int32 [96, 8192], P(None, 'space'), may hold values from -1 to 831, as said below
- emb_scale: float32 [4, 25], P('mp'), may hold values from -4 to 4
- emb_shift: float32 [4, 25], P('mp'), may hold values from -4 to 4
- emb_middle: bfloat16 [4, 50, 25], P('mp'), may hold values from -1.25 to 1.25
- emb_mid_bias: float32 [4, 50], P('mp'), may hold values from -3 to 3
- emb_outer: bfloat16 [4, 100, 50], P('mp'), may hold values from -0.875 to 0.875
- emb_out_bias: float32 [4, 100], P('mp'), may hold values from -3 to 3
- fit_first: bfloat16 [4, 240, 1600], P('mp'), may hold values from -0.078125 to 0.078125
- fit_first_bias: float32 [4, 240], P('mp'), may hold values from -3 to 3
- fit_second: bfloat16 [4, 240, 240], P('mp'), may hold values from -0.375 to 0.375
- fit_second_bias: float32 [4, 240], P('mp'), may hold values from -3 to 3
- fit_third: bfloat16 [4, 240, 240], P('mp'), may hold values from -0.375 to 0.375
- fit_third_bias: float32 [4, 240], P('mp'), may hold values from -3 to 3
- fit_readout: bfloat16 [4, 240], P('mp'), may hold values from -0.375 to 0.375
Outputs:
- mean_force: float32 [3, 128, 4, 16], P(None, 'space', 'mp')
- force_spread: float32 [128, 4, 16], P('space', 'mp')
- virial_spread: float32 [128, 4, 16], P('space', 'mp')
Inputs may be any that keep to these rules, and one draw needn't show every extreme that they name: `send_lists`: direction b runs +x, -x, +y, -y, +z, -z. A list of section b // 2 names owned atoms (below 64) or live ghost slots of earlier sections of the sender's extended array; live entries come first and -1 fills the rest; each list holds 42 to 128 live entries, entries may repeat, and in every draw some domain's list in each direction is full. `neighbours`: each entry names another owned atom of the same domain or a live ghost slot of that domain's extended array; -1 marks an empty slot.
All inputs are finite; a program needn't handle non-finite values.
Results may differ from a plain program's by a relative error of at most 0.012.
Values sent between devices are 32-bit elements; how exact they have to be, the bound alone decides.
No kernel may reach another device: no remote copies, remote signals or barrier semaphores. Data moves between devices by JAX's collectives and lax.ppermute only.
A program may use at most 64 MiB of HBM per device.

v0:
```python
import jax
import jax.numpy as jnp
from jax import lax
from jax.sharding import PartitionSpec as P

AXIS = 16
K = 96


SOFTEN = 0.04


def from_behind(value, axis, steps):
    count = lax.axis_size(axis)
    pairs = [(source, (source + steps) % count) for source in range(count)]
    return lax.ppermute(value, axis, pairs)


def sent_to_all(shard, axis):
    length = lax.axis_size(axis)
    return lax.all_to_all(
        jnp.broadcast_to(shard[None], (length, *shard.shape)), axis, 0, 0, tiled=True
    )


def taken_together(shard, axis):
    return sent_to_all(shard, axis).sum(axis=0)


def packed_total(arrays, axis):
    ends = [0]
    for a in arrays:
        ends.append(ends[-1] + a.size)
    total = taken_together(jnp.concatenate([a.ravel() for a in arrays]), axis)
    return tuple((total[b:e].reshape(a.shape) for a, b, e in zip(arrays, ends, ends[1:])))


def describe(pieces, embedding):
    offsets, present = pieces
    scale_in, shift_in, mat_two, bias_two, mat_three, bias_three = embedding
    radius_sq = jnp.sum(offsets * offsets, axis=0) + SOFTEN
    inverse = lax.rsqrt(radius_sq)
    scaled = inverse * inverse
    envelope = (
        jnp.stack([inverse, scaled * offsets[0], scaled * offsets[1], scaled * offsets[2]])
        * present[None]
    )
    flat_inv = inverse.reshape(1, -1)
    layer_one = jnp.tanh(scale_in[:, None] * flat_inv + shift_in[:, None]).astype(jnp.bfloat16)
    pre_two = jnp.dot(mat_two, layer_one, preferred_element_type=jnp.float32) + bias_two[:, None]
    layer_two = (
        jnp.concatenate([layer_one, layer_one], axis=0).astype(jnp.float32) + jnp.tanh(pre_two)
    ).astype(jnp.bfloat16)
    pre_three = (
        jnp.dot(mat_three, layer_two, preferred_element_type=jnp.float32) + bias_three[:, None]
    )
    layer_three = (
        jnp.concatenate([layer_two, layer_two], axis=0).astype(jnp.float32) + jnp.tanh(pre_three)
    ).astype(jnp.bfloat16)
    filters = layer_three.astype(jnp.float32).reshape(
        layer_three.shape[0], offsets.shape[1], offsets.shape[2]
    )
    moments = jnp.einsum("ckb,mkb->cmb", envelope, filters) / K
    feature = jnp.einsum("cmb,cnb->mnb", moments, moments[:, :AXIS])
    return feature.reshape(-1, offsets.shape[2]).astype(jnp.bfloat16)


def domain_energy(offsets, present, embedding, fitting):
    atom_count = offsets.shape[2]
    block_total = atom_count // atom_count
    shaped = offsets.reshape(3, K, block_total, atom_count).transpose(2, 0, 1, 3)
    present_blocks = present.reshape(K, block_total, atom_count).transpose(1, 0, 2)
    features = lax.map(lambda pieces: describe(pieces, embedding), (shaped, present_blocks))
    features = features.transpose(1, 0, 2).reshape(-1, atom_count)
    fit_one, fit_bias_one, fit_two, fit_bias_two, fit_three, fit_bias_three, readout = fitting
    hidden_one = jnp.tanh(
        jnp.dot(fit_one, features, preferred_element_type=jnp.float32) + fit_bias_one[:, None]
    ).astype(jnp.bfloat16)
    hidden_two = (
        hidden_one.astype(jnp.float32)
        + jnp.tanh(
            jnp.dot(fit_two, hidden_one, preferred_element_type=jnp.float32) + fit_bias_two[:, None]
        )
    ).astype(jnp.bfloat16)
    hidden_three = (
        hidden_two.astype(jnp.float32)
        + jnp.tanh(
            jnp.dot(fit_three, hidden_two, preferred_element_type=jnp.float32)
            + fit_bias_three[:, None]
        )
    ).astype(jnp.bfloat16)
    return jnp.sum(jnp.dot(readout, hidden_three, preferred_element_type=jnp.float32))


def domain_terms(extended, neighbour_ids, embedding, fitting):
    owned_count = neighbour_ids.shape[1]
    ext_len = extended.shape[1]
    present = neighbour_ids >= 0
    safe_ids = jnp.where(present, neighbour_ids, ext_len)
    gathered = jnp.take(extended, safe_ids, axis=1, mode="fill", fill_value=0.0)
    offsets = gathered - extended[:, None, :owned_count]
    present_f = present.astype(jnp.float32)
    energy, pullback = jax.vjp(
        lambda shifted: domain_energy(shifted, present_f, embedding, fitting), offsets
    )
    (gradient,) = pullback(jnp.ones((), jnp.float32))
    virial = -(offsets[:, None] * gradient[None, :]).reshape(9, K, owned_count)
    spread_terms = jnp.concatenate([-gradient, virial], axis=0).reshape(12, -1)
    totals = (
        jnp.zeros((12, ext_len), jnp.float32)
        .at[:, safe_ids.reshape(-1)]
        .add(spread_terms, mode="drop")
    )
    centre = jnp.sum(gradient, axis=1)
    return totals.at[0:3, :owned_count].add(centre)


def pick_columns(extended, chosen):
    safe_ids = jnp.where(chosen >= 0, chosen, extended.shape[1])
    return jnp.take(extended, safe_ids, axis=1, mode="fill", fill_value=0.0)


def add_columns(totals, chosen, values):
    safe_ids = jnp.where(chosen >= 0, chosen, totals.shape[1])
    return totals.at[:, safe_ids].add(values, mode="drop")


def local(
    positions,
    send_lists,
    neighbours,
    emb_scale,
    emb_shift,
    emb_middle,
    emb_mid_bias,
    emb_outer,
    emb_out_bias,
    fit_first,
    fit_first_bias,
    fit_second,
    fit_second_bias,
    fit_third,
    fit_third_bias,
    fit_readout,
):
    space_count = lax.axis_size("space")
    model_count = lax.axis_size("mp")
    grid_y = min(4, max(2, space_count // 16))
    strides = (grid_y * grid_y, grid_y, 1)
    my_lists = send_lists[0]
    capacity = my_lists.shape[1]
    owned_count = positions.shape[1]
    extended = positions
    for section_id in range(3):
        stride = strides[section_id]
        received = []
        for side_id in range(2):
            payload = pick_columns(extended, my_lists[2 * section_id + side_id])
            received.append(from_behind(payload, "space", stride if side_id == 0 else -stride))
        for side_id in range(2):
            offset_vec = (
                jnp.zeros((3, 1), jnp.float32).at[section_id, 0].set(-1.0 if side_id == 0 else 1.0)
            )
            extended = jnp.concatenate([extended, received[side_id] + offset_vec], axis=1)
    embedding = (
        emb_scale[0],
        emb_shift[0],
        emb_middle[0],
        emb_mid_bias[0],
        emb_outer[0],
        emb_out_bias[0],
    )
    fitting = (
        fit_first[0],
        fit_first_bias[0],
        fit_second[0],
        fit_second_bias[0],
        fit_third[0],
        fit_third_bias[0],
        fit_readout[0],
    )
    totals = domain_terms(extended, neighbours, embedding, fitting)
    for section_id in (2, 1, 0):
        stride = strides[section_id]
        returned = []
        for side_id in range(2):
            first_col = owned_count + (2 * section_id + side_id) * capacity
            ghost_block = totals[:, first_col : first_col + capacity]
            returned.append(from_behind(ghost_block, "space", -stride if side_id == 0 else stride))
        for side_id in range(2):
            totals = add_columns(totals, my_lists[2 * section_id + side_id], returned[side_id])
    owned_terms = totals[:, :owned_count]
    quarter = owned_count // model_count
    force_sq = jnp.sum(owned_terms[0:3] * owned_terms[0:3], axis=0)
    virial_sq = jnp.sum(owned_terms[3:12] * owned_terms[3:12], axis=0)
    summed, force_total, virial_total = packed_total((owned_terms, force_sq, virial_sq), "mp")
    mean_all = summed / model_count
    force_var = force_total / model_count - jnp.sum(mean_all[0:3] * mean_all[0:3], axis=0)
    virial_var = virial_total / model_count - jnp.sum(mean_all[3:12] * mean_all[3:12], axis=0)
    member = lax.axis_index("mp")
    mean_part = lax.dynamic_slice_in_dim(mean_all[0:3], member * quarter, quarter, axis=1)
    force_part = lax.dynamic_slice_in_dim(force_var, member * quarter, quarter)
    virial_part = lax.dynamic_slice_in_dim(virial_var, member * quarter, quarter)
    return (
        mean_part.reshape(3, 1, 1, quarter),
        force_part.reshape(1, 1, quarter),
        virial_part.reshape(1, 1, quarter),
    )


def solution(mesh):
    return jax.shard_map(
        local,
        mesh=mesh,
        in_specs=(
            P(None, "space"),
            P("space", None, None),
            P(None, "space"),
            P("mp", None),
            P("mp", None),
            P("mp", None, None),
            P("mp", None),
            P("mp", None, None),
            P("mp", None),
            P("mp", None, None),
            P("mp", None),
            P("mp", None, None),
            P("mp", None),
            P("mp", None, None),
            P("mp", None),
            P("mp", None),
        ),
        out_specs=(P(None, "space", "mp", None), P("space", "mp", None), P("space", "mp", None)),
        check_vma=False,
    )
```

profile of v0, /device:TPU:3, one launch (start us, length us, event | category | flops | bytes accessed | tf_op | source)
XLA Modules:
  0.0 239.9 jit_solution(2086847345316793512)
XLA Ops:
  0.7 0.8 compare_and_fusion.1
  1.5 0.8 copy.215
  3.0 4.9 %collective-permute-start = (f32[3,128]{0,1:T(8,128)S(1)}, f32[3,128]{0,1:T(8,128)S(1)}, u32[]{:S(2)}, u32[]{:S(2)}) collective-permute-start(f32[3,128]{0,1:T(8,128)S(1)} %select_bitcast_fusion.5), channel_id=1, source_target_pairs={{0,16},{1,17},{2,18},{3,19},{4,20},{5,21},{6,22},{7,23},{8,24},{9,... | collective-permute-start | bytes 4616 | tf_op jit(solution)/shard_map/ppermute | solution.py:16
  7.9 0.6 gather_fusion.2
  8.7 4.4 %collective-permute-start.1 = (f32[3,128]{0,1:T(8,128)S(1)}, f32[3,128]{0,1:T(8,128)S(1)}, u32[]{:S(2)}, u32[]{:S(2)}) collective-permute-start(f32[3,128]{0,1:T(8,128)S(1)} %select_bitcast_fusion.4), channel_id=1, source_target_pairs={{0,112},{1,113},{2,114},{3,115},{4,116},{5,117},{6,118},{7,119},{8... | collective-permute-start | bytes 4616 | tf_op jit(solution)/shard_map/ppermute | solution.py:16
  13.0 0.8 compare_convert_fusion
  13.8 0.8 compare_select_fusion.1
  15.7 0.7 reduce.15
  16.9 0.7 constant_dynamic-update-slice_fusion.1
  17.6 0.7 constant_dynamic-update-slice_fusion
  18.3 0.6 gather_fusion.4
  19.7 3.8 %collective-permute-start.2 = (f32[3,128]{0,1:T(8,128)S(1)}, f32[3,128]{0,1:T(8,128)S(1)}, u32[]{:S(2)}, u32[]{:S(2)}) collective-permute-start(f32[3,128]{0,1:T(8,128)S(1)} %select_bitcast_fusion.3), channel_id=1, source_target_pairs={{0,4},{1,5},{2,6},{3,7},{4,8},{5,9},{6,10},{7,11},{8,12},{9,13},{1... | collective-permute-start | bytes 4616 | tf_op jit(solution)/shard_map/ppermute | solution.py:16
  23.6 7.8 %collective-permute-start.3 = (f32[3,128]{0,1:T(8,128)S(1)}, f32[3,128]{0,1:T(8,128)S(1)}, u32[]{:S(2)}, u32[]{:S(2)}) collective-permute-start(f32[3,128]{0,1:T(8,128)S(1)} %select_bitcast_fusion.2), channel_id=1, source_target_pairs={{0,124},{1,125},{2,126},{3,127},{4,0},{5,1},{6,2},{7,3},{8,4},{9,5... | collective-permute-start | bytes 4616 | tf_op jit(solution)/shard_map/ppermute | solution.py:16
  31.5 1.3 collective-permute-done.3
  34.1 3.4 %collective-permute-start.4 = (f32[3,128]{0,1:T(8,128)S(1)}, f32[3,128]{0,1:T(8,128)S(1)}, u32[]{:S(2)}, u32[]{:S(2)}) collective-permute-start(f32[3,128]{0,1:T(8,128)S(1)} %select_bitcast_fusion.1), channel_id=1, source_target_pairs={{0,1},{1,2},{2,3},{3,4},{4,5},{5,6},{6,7},{7,8},{8,9},{9,10},{10,1... | collective-permute-start | bytes 4616 | tf_op jit(solution)/shard_map/ppermute | solution.py:16
  37.6 2.5 %collective-permute-start.5 = (f32[3,128]{0,1:T(8,128)S(1)}, f32[3,128]{0,1:T(8,128)S(1)}, u32[]{:S(2)}, u32[]{:S(2)}) collective-permute-start(f32[3,128]{0,1:T(8,128)S(1)} %select_bitcast_fusion), channel_id=1, source_target_pairs={{0,127},{1,0},{2,1},{3,2},{4,3},{5,4},{6,5},{7,6},{8,7},{9,8},{10,... | collective-permute-start | bytes 4616 | tf_op jit(solution)/shard_map/ppermute | solution.py:16
  40.2 3.0 %collective-permute-done.5 = f32[3,128]{0,1:T(8,128)S(1)} collective-permute-done((f32[3,128]{0,1:T(8,128)S(1)}, f32[3,128]{0,1:T(8,128)S(1)}, u32[]{:S(2)}, u32[]{:S(2)}) %collective-permute-start.5) | collective-permute-done | bytes 1568 | tf_op jit(solution)/shard_map/ppermute | solution.py:16
  43.2 21.0 %gather_fusion = f32[6144,3]{1,0:T(8,128)} fusion(f32[3,832]{0,1:T(8,128)S(1)} %add_dynamic-update-slice_fusion, s32[6144]{0:T(1024)S(1)} %broadcast_clamp_fusion), kind=kCustom, calls=%fused_computation.6 | custom fusion | bytes 172032 | tf_op jit(solution)/shard_map/jit(_take)/gather | solution.py:100
  64.3 3.1 %copy.218 = f32[96,64,3]{0,1,2:T(8,128)S(1)} copy(f32[96,64,3]{2,1,0:T(8,128)} %bitcast.209) | data formatting | bytes 147456 | tf_op jit(solution)/shard_map/jit(_take)/gather | solution.py:100
  67.6 0.7 slice_multiply_fusion.7
  68.5 1.6 add_convert_fusion.1
  70.1 1.8 add_convert_fusion
  71.9 2.6 %copy.220 = bf16[100,6144]{0,1:T(8,128)(2,1)} copy(bf16[100,6144]{1,0:T(8,128)(2,1)} %get-tuple-element.312) | data formatting | bytes 2457600 | tf_op jit(solution)/shard_map/jvp()/while/body/eval_jaxpr/convert_element_type | solution.py:59
  74.5 0.8 maximum_multiply_fusion
  75.9 2.7 %fusion.37 = bf16[4,100,64]{1,0,2:T(4,128)(2,1)S(1)} fusion(bf16[100,96,64]{0,2,1:T(8,128)(2,1)} %bitcast.207, bf16[4,96,64]{1,2,0:T(8,128)(2,1)S(1)} %maximum_multiply_fusion), kind=kOutput, calls=%fused_computation.59 | convolution fusion | flops 4966400 | bytes 1329152 | tf_op jit(solution)/shard_map/jvp()/while/body/eval_jaxpr/ckb,mkb->cmb/dot_general | solution.py:63
  78.7 1.0 fusion.30
  79.7 2.2 copy.223
  81.9 1.4 fusion.42
  83.3 1.7 fusion.41
  85.0 1.9 fusion.43
  87.0 2.1 fusion.15
  89.0 1.9 copy.224
  91.0 2.2 copy.225
  93.1 1.2 convolution_bitcast_fusion
  94.3 1.2 fusion.33
  95.5 2.7 %fusion.17 = f32[64,4,96]{2,1,0:T(4,128)S(1)} fusion(bf16[64,100,4]{1,2,0:T(4,128)(2,1)S(1)} %fusion.33, bf16[100,96,64]{0,2,1:T(8,128)(2,1)} %bitcast.208), kind=kOutput, calls=%fused_computation.39 | convolution fusion | flops 4915200 | bytes 1378304 | tf_op jit(solution)/shard_map/transpose(jvp())/while/body/eval_jaxpr/ckb,mkb->cmb/dot_general | solution.py:63
  98.9 1.7 slice_add_fusion
  100.6 2.2 copy.231
  103.4 0.7 slice_multiply_fusion.4
  104.1 3.9 %copy.230 = bf16[50,96,64]{2,1,0:T(8,128)(2,1)} copy(bf16[50,96,64]{0,1,2:T(8,128)(2,1)} %slice_add_fusion) | data formatting | bytes 1228800 | tf_op jit(solution)/shard_map/transpose(jvp())/while/body/eval_jaxpr/add_any | solution.py:58
  108.1 3.0 %add_any.77 = bf16[50,6144]{1,0:T(8,128)(2,1)} reshape(bf16[50,96,64]{2,1,0:T(8,128)(2,1)} %copy.230) | data formatting | bytes 1228800 | tf_op jit(solution)/shard_map/transpose(jvp())/while/body/eval_jaxpr/add_any | solution.py:58
  111.1 3.5 %copy.232 = f32[100,6144]{1,0:T(8,128)} copy(f32[100,6144]{0,1:T(8,128)} %bitcast.206) | data formatting | bytes 4915200 | tf_op jit(solution)/shard_map/transpose(jvp())/while/body/eval_jaxpr/convert_element_type | solution.py:59
  114.7 2.6 %fusion.5 = bf16[50,6144]{1,0:T(8,128)(2,1)S(1)} fusion(bf16[50,6144]{1,0:T(8,128)(2,1)} %add_any.77, f32[100,6144]{1,0:T(8,128)} %copy.232, f32[100,6144]{1,0:T(8,128)S(1)} %get-tuple-element.313, bf16[1,100,50]{1,2,0:T(8,128)(2,1)S(1)} %copy-done.15), kind=kOutput, calls=%fused_computation.22 | convolution fusion | flops 64512000 | bytes 6154000 | tf_op jit(solution)/shard_map/transpose(jvp())/while/body/eval_jaxpr/dot_general | solution.py:55
  117.4 0.7 fusion.27
  119.1 2.2 copy.235
  121.3 33.6 %scatter_custom_fusion = f32[12,832]{0,1:T(8,128)S(1)} fusion(s32[6144]{0:T(1024)} %bitcast.214, f32[6144,12]{1,0:T(8,128)} %copy.235, f32[]{:T(128)} %constant.350.clone.1), kind=kCustom, calls=%fused_computation.80 | custom fusion | flops 73728 | bytes 40448 | tf_op jit(solution)/shard_map/scatter-add | solution.py:112
  154.9 0.8 scatter-add.55
  155.7 1.9 collective-permute-start.7
  157.6 2.5 %collective-permute-start.6 = (f32[12,128]{0,1:T(8,128)S(1)}, f32[12,128]{0,1:T(8,128)S(1)}, u32[]{:S(2)}, u32[]{:S(2)}) collective-permute-start(f32[12,128]{0,1:T(8,128)S(1)} %get-tuple-element.267), channel_id=1, source_target_pairs={{0,127},{1,0},{2,1},{3,2},{4,3},{5,4},{6,5},{7,6},{8,7},{9,8},{10,... | collective-permute-start | bytes 18440 | tf_op jit(solution)/shard_map/ppermute | solution.py:16
  160.1 3.5 %collective-permute-done.6 = f32[12,128]{0,1:T(8,128)S(1)} collective-permute-done((f32[12,128]{0,1:T(8,128)S(1)}, f32[12,128]{0,1:T(8,128)S(1)}, u32[]{:S(2)}, u32[]{:S(2)}) %collective-permute-start.6) | collective-permute-done | bytes 6176 | tf_op jit(solution)/shard_map/ppermute | solution.py:16
  163.7 1.4 scatter_custom_fusion.1
  165.1 1.4 scatter_custom_fusion.2
  166.6 25.5 %collective-permute-start.8 = (f32[12,128]{0,1:T(8,128)S(1)}, f32[12,128]{0,1:T(8,128)S(1)}, u32[]{:S(2)}, u32[]{:S(2)}) collective-permute-start(f32[12,128]{0,1:T(8,128)S(1)} %get-tuple-element.265), channel_id=1, source_target_pairs={{0,124},{1,125},{2,126},{3,127},{4,0},{5,1},{6,2},{7,3},{8,4},{9,5... | collective-permute-start | bytes 18440 | tf_op jit(solution)/shard_map/ppermute | solution.py:16
  192.1 1.9 collective-permute-start.9
  194.0 1.4 scatter_custom_fusion.3
  195.5 7.9 %collective-permute-done.9 = f32[12,128]{0,1:T(8,128)S(1)} collective-permute-done((f32[12,128]{0,1:T(8,128)S(1)}, f32[12,128]{0,1:T(8,128)S(1)}, u32[]{:S(2)}, u32[]{:S(2)}) %collective-permute-start.9) | collective-permute-done | bytes 6176 | tf_op jit(solution)/shard_map/ppermute | solution.py:16
  203.4 1.4 scatter_custom_fusion.4
  204.9 1.9 collective-permute-start.10
  206.8 4.3 %collective-permute-start.11 = (f32[12,128]{0,1:T(8,128)S(1)}, f32[12,128]{0,1:T(8,128)S(1)}, u32[]{:S(2)}, u32[]{:S(2)}) collective-permute-start(f32[12,128]{0,1:T(8,128)S(1)} %get-tuple-element.262), channel_id=1, source_target_pairs={{0,16},{1,17},{2,18},{3,19},{4,20},{5,21},{6,22},{7,23},{8,24},{9,... | collective-permute-start | bytes 18440 | tf_op jit(solution)/shard_map/ppermute | solution.py:16
  211.1 1.4 scatter_custom_fusion.5
  212.5 2.3 collective-permute-done.11
  214.8 1.4 scatter_custom_fusion.6
  217.4 9.5 %all-to-all-start = ((f32[4,1,896]{2,1,0:T(1,128)}), f32[4,1,896]{2,1,0:T(1,128)S(1)}, u32[]{:S(2)}, u32[]{:S(2)}) async-start(f32[4,1,896]{2,1,0:T(1,128)} %broadcast_in_dim.153), calls=%async_computation | async-start | bytes 28672 | tf_op jit(solution)/shard_map/all_to_all | solution.py:21
  226.9 11.4 %all-to-all-done = f32[4,1,896]{2,1,0:T(1,128)S(1)} async-done(((f32[4,1,896]{2,1,0:T(1,128)}), f32[4,1,896]{2,1,0:T(1,128)S(1)}, u32[]{:S(2)}, u32[]{:S(2)}) %all-to-all-start) | async-done | bytes 14368 | tf_op jit(solution)/shard_map/all_to_all | solution.py:21
  (139 shorter events, 10.9 us)
Async XLA Ops:
  0.6 81.2 %copy-start = (bf16[1,240,1600]{2,1,0:T(8,128)(2,1)S(1)}, bf16[1,240,1600]{2,1,0:T(8,128)(2,1)}, u32[]{:S(2)}) copy-start(bf16[1,240,1600]{2,1,0:T(8,128)(2,1)} %param.45) | copy-start | bytes 2304004
  0.6 30.8 %copy-start.26 = (f32[3]{0:T(128)S(1)}, f32[3]{0:T(128)}, u32[]{:S(2)}) copy-start(f32[3]{0:T(128)} %constant.358.clone.1) | copy-start | bytes 40
  0.7 32.1 %copy-start.25 = (f32[3]{0:T(128)S(1)}, f32[3]{0:T(128)}, u32[]{:S(2)}) copy-start(f32[3]{0:T(128)} %constant.359.clone.1) | copy-start | bytes 40
  0.7 39.5 %copy-start.24 = (f32[3]{0:T(128)S(1)}, f32[3]{0:T(128)}, u32[]{:S(2)}) copy-start(f32[3]{0:T(128)} %constant.361.clone.1) | copy-start | bytes 40
  0.7 42.5 %copy-start.23 = (f32[3]{0:T(128)S(1)}, f32[3]{0:T(128)}, u32[]{:S(2)}) copy-start(f32[3]{0:T(128)} %constant.362.clone.1) | copy-start | bytes 40
  3.0 13.9 %collective-permute-start = (f32[3,128]{0,1:T(8,128)S(1)}, f32[3,128]{0,1:T(8,128)S(1)}, u32[]{:S(2)}, u32[]{:S(2)}) collective-permute-start(f32[3,128]{0,1:T(8,128)S(1)} %select_bitcast_fusion.5), channel_id=1, source_target_pairs={{0,16},{1,17},{2,18},{3,19},{4,20},{5,21},{6,22},{7,23},{8,24},{9,... | collective-permute-start | bytes 4616 | tf_op jit(solution)/shard_map/ppermute | solution.py:16
  8.7 9.0 %collective-permute-start.1 = (f32[3,128]{0,1:T(8,128)S(1)}, f32[3,128]{0,1:T(8,128)S(1)}, u32[]{:S(2)}, u32[]{:S(2)}) collective-permute-start(f32[3,128]{0,1:T(8,128)S(1)} %select_bitcast_fusion.4), channel_id=1, source_target_pairs={{0,112},{1,113},{2,114},{3,115},{4,116},{5,117},{6,118},{7,119},{8... | collective-permute-start | bytes 4616 | tf_op jit(solution)/shard_map/ppermute | solution.py:16
  13.8 60.7 %copy-start.5 = (f32[96,64]{0,1:T(8,128)}, f32[96,64]{0,1:T(8,128)S(1)}, u32[]{:S(2)}) copy-start(f32[96,64]{0,1:T(8,128)S(1)} %get-tuple-element.284) | copy-start | bytes 73732
  19.7 11.7 %collective-permute-start.2 = (f32[3,128]{0,1:T(8,128)S(1)}, f32[3,128]{0,1:T(8,128)S(1)}, u32[]{:S(2)}, u32[]{:S(2)}) collective-permute-start(f32[3,128]{0,1:T(8,128)S(1)} %select_bitcast_fusion.3), channel_id=1, source_target_pairs={{0,4},{1,5},{2,6},{3,7},{4,8},{5,9},{6,10},{7,11},{8,12},{9,13},{1... | collective-permute-start | bytes 4616 | tf_op jit(solution)/shard_map/ppermute | solution.py:16
  23.6 9.2 %collective-permute-start.3 = (f32[3,128]{0,1:T(8,128)S(1)}, f32[3,128]{0,1:T(8,128)S(1)}, u32[]{:S(2)}, u32[]{:S(2)}) collective-permute-start(f32[3,128]{0,1:T(8,128)S(1)} %select_bitcast_fusion.2), channel_id=1, source_target_pairs={{0,124},{1,125},{2,126},{3,127},{4,0},{5,1},{6,2},{7,3},{8,4},{9,5... | collective-permute-start | bytes 4616 | tf_op jit(solution)/shard_map/ppermute | solution.py:16
  34.1 6.0 %collective-permute-start.4 = (f32[3,128]{0,1:T(8,128)S(1)}, f32[3,128]{0,1:T(8,128)S(1)}, u32[]{:S(2)}, u32[]{:S(2)}) collective-permute-start(f32[3,128]{0,1:T(8,128)S(1)} %select_bitcast_fusion.1), channel_id=1, source_target_pairs={{0,1},{1,2},{2,3},{3,4},{4,5},{5,6},{6,7},{7,8},{8,9},{9,10},{10,1... | collective-permute-start | bytes 4616 | tf_op jit(solution)/shard_map/ppermute | solution.py:16
  37.6 5.6 %collective-permute-start.5 = (f32[3,128]{0,1:T(8,128)S(1)}, f32[3,128]{0,1:T(8,128)S(1)}, u32[]{:S(2)}, u32[]{:S(2)}) collective-permute-start(f32[3,128]{0,1:T(8,128)S(1)} %select_bitcast_fusion), channel_id=1, source_target_pairs={{0,127},{1,0},{2,1},{3,2},{4,3},{5,4},{6,5},{7,6},{8,7},{9,8},{10,... | collective-permute-start | bytes 4616 | tf_op jit(solution)/shard_map/ppermute | solution.py:16
  64.2 3.1 %copy-start.17 = (f32[3,64]{1,0:T(4,128)S(1)}, f32[3,64]{1,0:T(4,128)}, u32[]{:S(2)}) copy-start(f32[3,64]{1,0:T(4,128)} %param.36) | copy-start | bytes 2308
  64.2 4.1 %copy-start.19 = (f32[1,25]{1,0:T(1,128)S(1)}, f32[1,25]{1,0:T(1,128)}, u32[]{:S(2)}) copy-start(f32[1,25]{1,0:T(1,128)} %param.40) | copy-start | bytes 304
  64.2 4.1 %copy-start.21 = (f32[1,25]{1,0:T(1,128)S(1)}, f32[1,25]{1,0:T(1,128)}, u32[]{:S(2)}) copy-start(f32[1,25]{1,0:T(1,128)} %param.39) | copy-start | bytes 304
  64.2 4.3 %copy-start.27 = (bf16[1,50,25]{1,2,0:T(8,128)(2,1)S(1)}, bf16[1,50,25]{1,2,0:T(8,128)(2,1)}, u32[]{:S(2)}) copy-start(bf16[1,50,25]{1,2,0:T(8,128)(2,1)} %param.41) | copy-start | bytes 7504
  64.2 4.3 %copy-start.29 = (f32[1,50]{1,0:T(1,128)S(1)}, f32[1,50]{1,0:T(1,128)}, u32[]{:S(2)}) copy-start(f32[1,50]{1,0:T(1,128)} %param.42) | copy-start | bytes 604
  67.6 2.5 %copy-start.12 = (f32[6144]{0:T(1024)}, f32[6144]{0:T(1024)S(1)}, u32[]{:S(2)}) copy-start(f32[6144]{0:T(1024)S(1)} %rsqrt.32) | copy-start | bytes 73732
  68.3 1.8 copy-start.14
  68.3 1.8 copy-start.18
  75.3 0.6 copy-start.7
  78.7 3.2 %copy-start.3 = (bf16[4,100,64]{1,0,2:T(4,128)(2,1)}, bf16[4,100,64]{1,0,2:T(4,128)(2,1)S(1)}, u32[]{:S(2)}) copy-start(bf16[4,100,64]{1,0,2:T(4,128)(2,1)S(1)} %fusion.37) | copy-start | bytes 153604
  89.0 5.3 %copy-start.4 = (bf16[4,100,64]{1,0,2:T(4,128)(2,1)S(1)}, bf16[4,100,64]{1,0,2:T(4,128)(2,1)}, u32[]{:S(2)}) copy-start(bf16[4,100,64]{1,0,2:T(4,128)(2,1)} %copy-done.3) | copy-start | bytes 153604
  93.1 5.1 %copy-start.8 = (bf16[4,96,64]{1,2,0:T(8,128)(2,1)S(1)}, bf16[4,96,64]{1,2,0:T(8,128)(2,1)}, u32[]{:S(2)}) copy-start(bf16[4,96,64]{1,2,0:T(8,128)(2,1)} %copy-done.7) | copy-start | bytes 147460
  100.6 2.2 copy-start.6
  102.8 0.7 copy-start.1
  111.1 3.5 %copy-start.15 = (bf16[1,100,50]{1,2,0:T(8,128)(2,1)S(1)}, bf16[1,100,50]{1,2,0:T(8,128)(2,1)}, u32[]{:S(2)}) copy-start(bf16[1,100,50]{1,2,0:T(8,128)(2,1)} %param.43) | copy-start | bytes 30004
  114.6 2.7 %copy-start.13 = (f32[6144]{0:T(1024)S(1)}, f32[6144]{0:T(1024)}, u32[]{:S(2)}) copy-start(f32[6144]{0:T(1024)} %copy-done.12) | copy-start | bytes 73732
  114.6 2.7 %copy-start.20 = (f32[1,25]{1,0:T(1,128)S(1)}, f32[1,25]{1,0:T(1,128)}, u32[]{:S(2)}) copy-start(f32[1,25]{1,0:T(1,128)} %param.40) | copy-start | bytes 304
  114.6 2.7 %copy-start.22 = (f32[1,25]{1,0:T(1,128)S(1)}, f32[1,25]{1,0:T(1,128)}, u32[]{:S(2)}) copy-start(f32[1,25]{1,0:T(1,128)} %param.39) | copy-start | bytes 304
  114.6 2.7 %copy-start.28 = (bf16[1,50,25]{1,2,0:T(8,128)(2,1)S(1)}, bf16[1,50,25]{1,2,0:T(8,128)(2,1)}, u32[]{:S(2)}) copy-start(bf16[1,50,25]{1,2,0:T(8,128)(2,1)} %param.41) | copy-start | bytes 7504
  114.7 2.7 %copy-start.30 = (f32[50,6144]{1,0:T(8,128)S(1)}, f32[50,6144]{1,0:T(8,128)}, u32[]{:S(2)}) copy-start(f32[50,6144]{1,0:T(8,128)} %get-tuple-element.311) | copy-start | bytes 3686404
  117.3 0.9 copy-start.2
  117.4 0.9 copy-start.9
  117.4 0.9 copy-start.10
  117.4 0.9 copy-start.11
  119.0 41.1 %copy-start.16 = (s32[1,6,128]{2,0,1:T(1,128)S(1)}, s32[1,6,128]{2,0,1:T(1,128)}, u32[]{:S(2)}) copy-start(s32[1,6,128]{2,0,1:T(1,128)} %param.37) | copy-start | bytes 9220
  155.7 9.4 %collective-permute-start.7 = (f32[12,128]{0,1:T(8,128)S(1)}, f32[12,128]{0,1:T(8,128)S(1)}, u32[]{:S(2)}, u32[]{:S(2)}) collective-permute-start(f32[12,128]{0,1:T(8,128)S(1)} %get-tuple-element.266), channel_id=1, source_target_pairs={{0,1},{1,2},{2,3},{3,4},{4,5},{5,6},{6,7},{7,8},{8,9},{9,10},{10,1... | collective-permute-start | bytes 18440 | tf_op jit(solution)/shard_map/ppermute | solution.py:16
  157.6 6.0 %collective-permute-start.6 = (f32[12,128]{0,1:T(8,128)S(1)}, f32[12,128]{0,1:T(8,128)S(1)}, u32[]{:S(2)}, u32[]{:S(2)}) collective-permute-start(f32[12,128]{0,1:T(8,128)S(1)} %get-tuple-element.267), channel_id=1, source_target_pairs={{0,127},{1,0},{2,1},{3,2},{4,3},{5,4},{6,5},{7,6},{8,7},{9,8},{10,... | collective-permute-start | bytes 18440 | tf_op jit(solution)/shard_map/ppermute | solution.py:16
  166.6 27.5 %collective-permute-start.8 = (f32[12,128]{0,1:T(8,128)S(1)}, f32[12,128]{0,1:T(8,128)S(1)}, u32[]{:S(2)}, u32[]{:S(2)}) collective-permute-start(f32[12,128]{0,1:T(8,128)S(1)} %get-tuple-element.265), channel_id=1, source_target_pairs={{0,124},{1,125},{2,126},{3,127},{4,0},{5,1},{6,2},{7,3},{8,4},{9,5... | collective-permute-start | bytes 18440 | tf_op jit(solution)/shard_map/ppermute | solution.py:16
  192.1 11.3 %collective-permute-start.9 = (f32[12,128]{0,1:T(8,128)S(1)}, f32[12,128]{0,1:T(8,128)S(1)}, u32[]{:S(2)}, u32[]{:S(2)}) collective-permute-start(f32[12,128]{0,1:T(8,128)S(1)} %get-tuple-element.264), channel_id=1, source_target_pairs={{0,4},{1,5},{2,6},{3,7},{4,8},{5,9},{6,10},{7,11},{8,12},{9,13},{1... | collective-permute-start | bytes 18440 | tf_op jit(solution)/shard_map/ppermute | solution.py:16
  204.9 6.2 %collective-permute-start.10 = (f32[12,128]{0,1:T(8,128)S(1)}, f32[12,128]{0,1:T(8,128)S(1)}, u32[]{:S(2)}, u32[]{:S(2)}) collective-permute-start(f32[12,128]{0,1:T(8,128)S(1)} %get-tuple-element.263), channel_id=1, source_target_pairs={{0,112},{1,113},{2,114},{3,115},{4,116},{5,117},{6,118},{7,119},{8... | collective-permute-start | bytes 18440 | tf_op jit(solution)/shard_map/ppermute | solution.py:16
  206.8 8.0 %collective-permute-start.11 = (f32[12,128]{0,1:T(8,128)S(1)}, f32[12,128]{0,1:T(8,128)S(1)}, u32[]{:S(2)}, u32[]{:S(2)}) collective-permute-start(f32[12,128]{0,1:T(8,128)S(1)} %get-tuple-element.262), channel_id=1, source_target_pairs={{0,16},{1,17},{2,18},{3,19},{4,20},{5,21},{6,22},{7,23},{8,24},{9,... | collective-permute-start | bytes 18440 | tf_op jit(solution)/shard_map/ppermute | solution.py:16
  217.4 20.9 %all-to-all-start = ((f32[4,1,896]{2,1,0:T(1,128)}), f32[4,1,896]{2,1,0:T(1,128)S(1)}, u32[]{:S(2)}, u32[]{:S(2)}) async-start(f32[4,1,896]{2,1,0:T(1,128)} %broadcast_in_dim.153), calls=%async_computation | async-start | bytes 28672 | tf_op jit(solution)/shard_map/all_to_all | solution.py:21
where the time goes:
time: 241 us; the launch traced here: 240 us
  starting transfers between devices  74.3 us (31%)
  local copies, waits for them, and re-layouts  58.1 us (24%)
  other arithmetic  53.2 us (22%)
  waiting for transfers between devices  29.5 us (12%)
  matrix products  23.3 us (10%)
    ppermute x12, starting transfers between devices, from_behind(): return lax.ppermute(value, axis, pairs)  64.8 us
    scatter-add x1, other arithmetic, domain_terms(): totals = jnp.zeros((12, ext_len), jnp.float32).at[:, safe_ids.reshape(-1)...  33.6 us
    gather x2, local copies, waits for them, and re-layouts, domain_terms(): gathered = jnp.take(extended, safe_ids, axis=1, mode='fill', fill_value=0.0)  24.1 us
    ppermute x12, waiting for transfers between devices, from_behind(): return lax.ppermute(value, axis, pairs)  18.1 us
    all_to_all x1, waiting for transfers between devices, sent_to_all(): lax.all_to_all(jnp.broadcast_to(shard[None], (length, *shard.shape)), axi...  11.4 us
    all_to_all x1, starting transfers between devices, sent_to_all(): lax.all_to_all(jnp.broadcast_to(shard[None], (length, *shard.shape)), axi...  9.53 us
    scatter-add x6, other arithmetic, add_columns(): return totals.at[:, safe_ids].add(values, mode='drop')  8.54 us
    convert_element_type x3, local copies, waits for them, and re-layouts, describe(): layer_three = (jnp.concatenate([layer_two, layer_two], axis=0).astype(jnp...  8.31 us
  transfers between devices with their start and end apart: 13, of which 6 were waited for; matrix products, arithmetic and copies ran while one was open for 4% of the time, Pallas kernels for 0%

commit v1 on v0

v1 whole, which is shorter than its diff:
```python
import jax
import jax.numpy as jnp
from jax import lax
from jax.experimental import pallas as pl
from jax.experimental.pallas import tpu as pltpu
from jax.sharding import PartitionSpec as P

F32, BF16, I32 = jnp.float32, jnp.bfloat16, jnp.int32
K = 96
ROWS = K // 2
SOFTEN = 0.04
RUN = 8
SPAN = 3
OFFSETS = tuple((a, b, c) for a in (-1, 0, 1) for b in (-1, 0, 1) for c in (-1, 0, 1))


def slot_of(a, b, c):
    return (a + 1) * 9 + (b + 1) * 3 + (c + 1)


def step_of(a, b, c):
    return 16 * a + 4 * b + c


def place_of(a, b, c):
    return (3 if 4 * b + c <= -3 else 0) + a + 1


def iota(shape, dim):
    return lax.broadcasted_iota(I32, shape, dim)


def lanes_of(table, index):
    return jnp.take_along_axis(table, index, axis=1, mode="promise_in_bounds")


def across(row, count):
    return jnp.broadcast_to(row, (count, row.shape[1]))


def half_turn(x):
    return pltpu.roll(x, 64, axis=x.ndim - 1)


def dot(a, b):
    return jnp.dot(a, b, preferred_element_type=F32)


def dot_last(a, b):
    return lax.dot_general(a, b, (((1,), (1,)), ((), ())), preferred_element_type=F32)


def outgoing(lists_ref, pos_ref, out_ref):
    count = out_ref.shape[0]
    me = lax.axis_index("space")
    lists = lists_ref[0].astype(F32)
    pos = pos_ref[...]
    row_xy = jnp.concatenate([pos[0:1], pos[1:2]], axis=1)
    row_z = jnp.concatenate([pos[2:3], pos[2:3]], axis=1)
    for a, b, c in OFFSETS:
        target = lax.rem(me + step_of(a, b, c) + count, count)
        block = next((2 * s + (0 if v > 0 else 1) for s, v in enumerate((a, b, c)) if v), None)
        first = jnp.zeros((1, 128), F32) if block is None else lists[block : block + 1]
        out_ref[target, :, 0:128] = first
        out_ref[target, :, 128:256] = row_xy
        out_ref[target, :, 256:384] = row_z


def grouped(rows, cols, by_row):
    r, c = iota((rows, cols), 0), iota((rows, cols), 1)
    wide, narrow = (r, c) if by_row else (c, r)
    hit = (narrow == (wide // 32) * 25 + wide % 32) & (wide % 32 < 25)
    return hit.astype(F32).astype(BF16)


def eye(n):
    return (iota((n, n), 0) == iota((n, n), 1)).astype(F32).astype(BF16)


def weights(
    scale_ref, shift_ref, mid_ref, mid_b_ref, outer_ref, outer_b_ref,
    one_ref, one_b_ref, two_ref, two_b_ref, three_ref, three_b_ref, read_ref,
    w2_ref, w2t_ref, w3_ref, w3t_ref, cols_ref, ecols_ref, f1_ref, f1t_ref, f2t_ref, f3t_ref,
    stack_ref,
):
    w2 = dot(dot(grouped(64, 50, True), mid_ref[0]).astype(BF16), grouped(25, 32, False)).astype(BF16)
    w3 = dot(dot(grouped(128, 100, True), outer_ref[0]).astype(BF16), grouped(50, 64, False)).astype(BF16)
    w2_ref[...] = w2
    w3_ref[...] = w3
    w2t_ref[...] = dot_last(eye(32), w2).astype(BF16)
    w3t_ref[...] = dot_last(eye(64), w3).astype(BF16)
    f2t_ref[...] = dot_last(eye(240), two_ref[0]).astype(BF16)
    f3t_ref[...] = dot_last(eye(240), three_ref[0]).astype(BF16)
    stack_ref[...] = jnp.zeros_like(stack_ref)
    small = (scale_ref, shift_ref, mid_b_ref, outer_b_ref, one_b_ref, two_b_ref, three_b_ref, read_ref)
    for i, ref in enumerate(small):
        stack_ref[i : i + 1, 0 : ref.shape[1]] = ref[...].astype(F32)
    turned = jnp.transpose(stack_ref[...], (1, 0))
    cols_ref[...] = turned
    ecols_ref[...] = jnp.zeros_like(ecols_ref)
    for q in range(4):
        ecols_ref[32 * q : 32 * q + 25, :] = turned[25 * q : 25 * q + 25]
    f1t_ref[...] = jnp.zeros_like(f1t_ref)
    for part in range(2):
        r, c = iota((256, 128), 0), iota((256, 128), 1)
        pick = (r == (c % 16) * 16 + c // 16 + 8 * part).astype(F32).astype(BF16)
        r, c = iota((128, 256), 0), iota((128, 256), 1)
        pick_t = (c == (r % 16) * 16 + r // 16 + 8 * part).astype(F32).astype(BF16)
        for blk in range(7):
            wide = min(256, 1600 - 256 * blk)
            piece = one_ref[0, :, 256 * blk : 256 * blk + wide]
            f1_ref[240 * part : 240 * part + 240, 128 * blk : 128 * blk + 128] = dot(
                piece, pick[0:wide]
            ).astype(BF16)
            f1t_ref[128 * blk : 128 * blk + 128, 256 * part : 256 * part + 240] = dot_last(
                pick_t[:, 0:wide], piece
            ).astype(BF16)


def resolve(me, count, recv_ref, num_ref, ext_ref, code_ref):
    def source(a, b, c):
        return lax.rem(me - step_of(a, b, c) + count, count)

    def listed(a, b, c):
        return recv_ref[source(a, b, c), :, 0:128].astype(I32)

    def coded(a, b, c):
        return listed(a, b, c) + 64 * slot_of(a, b, c)

    num_ref[...] = jnp.zeros_like(num_ref)
    pairs = [(b, c) for b in (1, -1) for c in (-1, 0, 1)]
    for i, (b, c) in enumerate(pairs):
        entry = listed(0, b, c)
        num_ref[0, i : i + 1] = entry
        num_ref[1, i : i + 1] = entry + 64 * slot_of(0, b, c)
        num_ref[2, i : i + 1] = coded(1, b, c)
        num_ref[3, i : i + 1] = coded(-1, b, c)
    entry = num_ref[0]
    index = (entry + 64) & 127
    middle = jnp.where(
        entry < 64,
        num_ref[1],
        jnp.where(entry < 192, lanes_of(num_ref[2], index), lanes_of(num_ref[3], index)),
    )
    num_ref[4] = middle
    for i, c in enumerate((1, -1)):
        entry = listed(0, 0, c)
        num_ref[5, i : i + 1] = entry
        num_ref[6, i : i + 1] = entry + 64 * slot_of(0, 0, c)
        num_ref[7, i : i + 1] = coded(1, 0, c)
        num_ref[8, i : i + 1] = coded(-1, 0, c)
        num_ref[9, i : i + 1] = num_ref[4, c + 1 : c + 2]
        num_ref[10, i : i + 1] = num_ref[4, c + 4 : c + 5]
    entry = num_ref[5]
    index = (entry + 64) & 127
    found = num_ref[6]
    for i, least in enumerate((64, 192, 320, 448)):
        found = jnp.where(entry < least, found, lanes_of(num_ref[7 + i], index))
    num_ref[11] = found
    code_ref[0:1] = 64 * slot_of(0, 0, 0) + (iota((1, 128), 1) & 63)
    code_ref[1:2] = coded(1, 0, 0)
    code_ref[2:3] = coded(-1, 0, 0)
    code_ref[3:4] = num_ref[4, 1:2]
    code_ref[4:5] = num_ref[4, 4:5]
    code_ref[5:7] = num_ref[11, 0:2]
    code_ref[7:8] = jnp.zeros((1, 128), I32)
    code = code_ref[...]
    atom = code & 63
    owner = code >> 6
    spots = [jnp.zeros((8, 128), F32)] * 3
    for a, b, c in OFFSETS:
        e = source(a, b, c)
        row_xy = across(recv_ref[e, :, 128:256], 8)
        row_z = across(recv_ref[e, :, 256:384], 8)
        here = owner == slot_of(a, b, c)
        got = (lanes_of(row_xy, atom), lanes_of(row_xy, atom + 64), lanes_of(row_z, atom))
        spots = [jnp.where(here, g - float(o), s) for g, o, s in zip(got, (a, b, c), spots)]
    for i in range(3):
        ext_ref[i] = spots[i]


def evaluate(
    recv_ref, nb_ref, w2_ref, w2t_ref, w3_ref, w3t_ref, cols_ref, ecols_ref,
    f1_ref, f1t_ref, f2_ref, f2t_ref, f3_ref, f3t_ref,
    out_ref,
    num_ref, ext_ref, code_ref, idx_ref, off_ref, inv_ref, env_ref, hi_ref, lo_ref,
    s1_ref, s2_ref, s3_ref, h3_ref, mom_ref, nat_ref, axis_ref, feat_ref, dfeat_ref,
    dnat_ref, dmom_ref, denv_ref, dinv_ref, grad_ref, acc_ref,
):
    count = recv_ref.shape[0]
    me = lax.axis_index("space")
    resolve(me, count, recv_ref, num_ref, ext_ref, code_ref)

    idx_ref[:, 0:64] = nb_ref[0:ROWS, :]
    idx_ref[:, 64:128] = nb_ref[ROWS:K, :]
    for q in range(ROWS // 8):
        at = slice(8 * q, 8 * q + 8)
        ids = idx_ref[at]
        present = jnp.where(ids >= 0, 1.0, 0.0)
        row, lane = (ids + 64) >> 7, (ids + 64) & 127
        spots = [jnp.zeros((8, 128), F32)] * 3
        code = jnp.zeros((8, 128), I32)
        for k in range(7):
            here = row == k
            spots = [
                jnp.where(here, lanes_of(across(ext_ref[i, k : k + 1], 8), lane), s)
                for i, s in enumerate(spots)
            ]
            code = jnp.where(here, lanes_of(across(code_ref[k : k + 1], 8), lane), code)
        offs = [s - ext_ref[i, 0:1] for i, s in enumerate(spots)]
        inverse = lax.rsqrt(offs[0] * offs[0] + offs[1] * offs[1] + offs[2] * offs[2] + SOFTEN)
        inv_ref[at] = inverse
        env_ref[0, at] = inverse * present
        for i in range(3):
            off_ref[i, at] = offs[i]
            env_ref[i + 1, at] = (inverse * inverse) * offs[i] * present
        hi_ref[at] = jnp.where(ids >= 0, code >> 7, -1)
        lo_ref[at] = code & 127

    mom_ref[...] = jnp.zeros_like(mom_ref)
    scale = jnp.broadcast_to(ecols_ref[0:32, 0:1], (32, 128))
    shift = jnp.broadcast_to(ecols_ref[0:32, 1:2], (32, 128))
    bias_two = jnp.concatenate([jnp.broadcast_to(ecols_ref[0:64, 2:3], (64, 128))] * 8, axis=1)
    bias_three = jnp.concatenate([jnp.broadcast_to(ecols_ref[0:128, 3:4], (128, 128))] * 8, axis=1)

    def forward(q, carry):
        base = pl.multiple_of(q * 8, 8)
        firsts = []
        for r in range(8):
            t = jnp.tanh(scale * inv_ref[pl.ds(base + r, 1), :] + shift)
            s1_ref[base + r] = (1.0 - t * t).astype(BF16)
            firsts.append(t.astype(BF16))
        h1 = jnp.concatenate(firsts, axis=1)
        t2 = jnp.tanh(dot(w2_ref[...], h1) + bias_two)
        h2 = (jnp.concatenate([h1, h1], axis=0).astype(F32) + t2).astype(BF16)
        s2 = (1.0 - t2 * t2).astype(BF16)
        t3 = jnp.tanh(dot(w3_ref[...], h2) + bias_three)
        h3 = (jnp.concatenate([h2, h2], axis=0).astype(F32) + t3).astype(BF16)
        s3 = (1.0 - t3 * t3).astype(BF16)
        for r in range(8):
            part = slice(128 * r, 128 * r + 128)
            s2_ref[base + r] = s2[:, part]
            s3_ref[base + r] = s3[:, part]
            h3_ref[base + r] = h3[:, part]
        for n in range(8):
            rows = slice(16 * n, 16 * n + 16)
            tiles = [h3[rows, 128 * r : 128 * r + 128].astype(F32) for r in range(8)]
            for c in range(4):
                total = tiles[0] * env_ref[c, pl.ds(base, 1), :]
                for r in range(1, 8):
                    total = total + tiles[r] * env_ref[c, pl.ds(base + r, 1), :]
                mom_ref[c, rows] = mom_ref[c, rows] + total
        return carry

    lax.fori_loop(0, ROWS // 8, forward, 0)

    low = iota((1, 128), 1) < 64
    nat_ref[:, 96:112, :] = jnp.zeros((4, 16, 128), F32)
    for c in range(4):
        m = mom_ref[c]
        m = (m + half_turn(m)) * (1.0 / K)
        for q in range(4):
            nat_ref[c, 25 * q : 25 * q + 25] = m[32 * q : 32 * q + 25]
        axis_ref[c] = jnp.where(low, m[0:8], m[8:16])
    for blk in range(7):
        mine = [nat_ref[c, 16 * blk : 16 * blk + 16] for c in range(4)]
        for p in range(8):
            total = mine[0] * axis_ref[0, p : p + 1]
            for c in range(1, 4):
                total = total + mine[c] * axis_ref[c, p : p + 1]
            feat_ref[128 * blk + 16 * p : 128 * blk + 16 * p + 16] = total.astype(BF16)

    both = dot(f1_ref[...], feat_ref[...])
    pre = jnp.where(low, both[0:240], both[240:480])
    t1 = jnp.tanh(pre + half_turn(pre) + cols_ref[0:240, 4:5])
    g1 = t1.astype(BF16)
    t2 = jnp.tanh(dot(f2_ref[0], g1) + cols_ref[0:240, 5:6])
    g2 = (g1.astype(F32) + t2).astype(BF16)
    t3 = jnp.tanh(dot(f3_ref[0], g2) + cols_ref[0:240, 6:7])
    d3 = jnp.broadcast_to(cols_ref[0:240, 7:8], (240, 128))
    back = dot(f3t_ref[...], (d3 * (1.0 - t3 * t3)).astype(BF16)).astype(BF16).astype(F32)
    d2 = (back + d3).astype(BF16).astype(F32)
    back = dot(f2t_ref[...], (d2 * (1.0 - t2 * t2)).astype(BF16)).astype(BF16).astype(F32)
    d1 = (back + d2).astype(BF16).astype(F32)
    d1 = d1 * (1.0 - t1 * t1)
    none = jnp.zeros((16, 128), F32)
    split = jnp.concatenate([jnp.where(low, d1, 0.0), none, jnp.where(low, 0.0, d1), none], axis=0)
    dfeat_ref[...] = dot(f1t_ref[...], split.astype(BF16)).astype(BF16).astype(F32)

    dmom_ref[...] = jnp.zeros_like(dmom_ref)
    for c in range(4):
        sums = [jnp.zeros((16, 128), F32)] * 8
        for blk in range(7):
            mine = nat_ref[c, 16 * blk : 16 * blk + 16]
            total = jnp.zeros((16, 128), F32)
            for p in range(8):
                d = dfeat_ref[128 * blk + 16 * p : 128 * blk + 16 * p + 16]
                total = total + d * axis_ref[c, p : p + 1]
                sums[p] = sums[p] + d * mine
            dnat_ref[c, 16 * blk : 16 * blk + 16] = total + half_turn(total)
        rows = jnp.concatenate([jnp.sum(s, axis=0, keepdims=True) for s in sums], axis=0)
        turned = half_turn(rows)
        dnat_ref[c, 0:8] = dnat_ref[c, 0:8] + jnp.where(low, rows, turned)
        dnat_ref[c, 8:16] = dnat_ref[c, 8:16] + jnp.where(low, turned, rows)
        for q in range(4):
            dmom_ref[c, 32 * q : 32 * q + 25] = dnat_ref[c, 25 * q : 25 * q + 25] * (1.0 / K)

    def backward(q, carry):
        base = pl.multiple_of(q * 8, 8)
        outer, pushed = [], []
        for r in range(8):
            env = [env_ref[c, pl.ds(base + r, 1), :] for c in range(4)]
            parts = [jnp.zeros((16, 128), F32)] * 4
            tiles = []
            for n in range(8):
                rows = slice(16 * n, 16 * n + 16)
                dm = [dmom_ref[c, rows] for c in range(4)]
                tiles.append((dm[0] * env[0] + dm[1] * env[1] + dm[2] * env[2] + dm[3] * env[3]).astype(BF16))
                h = h3_ref[base + r, rows].astype(F32)
                parts = [s + dm[c] * h for c, s in enumerate(parts)]
            for c in range(4):
                denv_ref[c, pl.ds(base + r, 1), :] = jnp.sum(parts[c], axis=0, keepdims=True)
            d = jnp.concatenate(tiles, axis=0)
            outer.append(d)
            pushed.append((d.astype(F32) * s3_ref[base + r].astype(F32)).astype(BF16))
        d3 = jnp.concatenate(outer, axis=1)
        back = dot(w3t_ref[...], jnp.concatenate(pushed, axis=1)).astype(BF16).astype(F32)
        d2 = (back + d3[0:64].astype(F32) + d3[64:128].astype(F32)).astype(BF16)
        s2 = jnp.concatenate([s2_ref[base + r] for r in range(8)], axis=1)
        back = dot(w2t_ref[...], (d2.astype(F32) * s2.astype(F32)).astype(BF16)).astype(BF16).astype(F32)
        d1 = (back + d2[0:32].astype(F32) + d2[32:64].astype(F32)).astype(BF16).astype(F32)
        for r in range(8):
            d = d1[:, 128 * r : 128 * r + 128] * s1_ref[base + r].astype(F32) * scale
            dinv_ref[pl.ds(base + r, 1), :] = jnp.sum(d, axis=0, keepdims=True)
        return carry

    lax.fori_loop(0, ROWS // 8, backward, 0)

    centre = [jnp.zeros((8, 128), F32)] * 3
    for q in range(ROWS // 8):
        at = slice(8 * q, 8 * q + 8)
        inverse = inv_ref[at]
        present = jnp.where(idx_ref[at] >= 0, 1.0, 0.0)
        offs = [off_ref[i, at] for i in range(3)]
        denv = [denv_ref[c, at] * present for c in range(4)]
        along = denv[1] * offs[0] + denv[2] * offs[1] + denv[3] * offs[2]
        square = inverse * inverse
        slope = (dinv_ref[at] + denv[0] + 2.0 * inverse * along) * (square * inverse) * -1.0
        for i in range(3):
            g = denv[i + 1] * square + slope * offs[i]
            grad_ref[i, at] = g
            centre[i] = centre[i] + g

    acc_ref[...] = jnp.zeros_like(acc_ref)
    which = iota((8, 128), 0)
    lead, next_up, rest = which % 3 == 0, which % 3 == 1, which >= 6
    spot = iota((128, 128), 0)

    def scatter(q, carry):
        base = pl.multiple_of(q * 8, 8)
        left, right = [], []
        for r in range(8):
            at = pl.ds(base + r, 1)
            gx, gy, gz = (across(grad_ref[i, at, :], 8) for i in range(3))
            ox, oy, oz = (across(off_ref[i, at, :], 8) for i in range(3))
            g_even = jnp.where(lead, gx, jnp.where(next_up, gz, gy))
            o_even = jnp.where((which < 2) | rest, 1.0, jnp.where(which == 2, ox, jnp.where(which < 5, oy, oz)))
            g_odd = jnp.where(lead, gy, jnp.where(next_up, gx, gz))
            o_odd = jnp.where((which < 1) | rest, 1.0, jnp.where(which < 3, ox, jnp.where(which < 4, oy, oz)))
            halves = (-g_even * o_even, -g_odd * o_odd)
            term = jnp.concatenate([jnp.where(rest, t - t.astype(BF16).astype(F32), t) for t in halves], axis=0)
            high = across(hi_ref[at, :], 16)
            left.append(jnp.concatenate([jnp.where(high == h, term, 0.0).astype(BF16) for h in range(14)], axis=0))
            right.append(jnp.where(spot == lo_ref[at, :], 1.0, 0.0).astype(BF16))
        acc_ref[...] = acc_ref[...] + dot_last(jnp.concatenate(left, axis=1), jnp.concatenate(right, axis=1))
        return carry

    lax.fori_loop(0, ROWS // 8, scatter, 0)

    rows = [jnp.sum(s, axis=0, keepdims=True) for s in centre]
    rows = [s + half_turn(s) for s in rows]
    own = jnp.concatenate(
        [jnp.where(low, rows[0], rows[1]), jnp.where(low, rows[2], 0.0), jnp.zeros((6, 128), F32)], axis=0
    )
    mine = me & (RUN - 1)
    for a, b, c in OFFSETS:
        h, odd = divmod(slot_of(a, b, c), 2)
        even_terms = acc_ref[16 * h : 16 * h + 8]
        odd_terms = acc_ref[16 * h + 8 : 16 * h + 16]
        even_terms = even_terms + jnp.where(which < 2, pltpu.roll(even_terms, 2, axis=0), 0.0)
        odd_terms = odd_terms + jnp.where(which < 1, pltpu.roll(odd_terms, 2, axis=0), 0.0)
        if odd:
            tile = jnp.where(low, half_turn(even_terms), odd_terms)
        else:
            tile = jnp.where(low, even_terms, half_turn(odd_terms))
        if (a, b, c) == (0, 0, 0):
            tile = tile + own
        place = 8 * place_of(a, b, c)
        out_ref[(mine - (4 * b + c)) & (RUN - 1), place : place + 8, :] = tile


def regroup(recv_ref, out_ref, sum_ref):
    me = lax.axis_index("space")
    mine, run = me & (RUN - 1), me // RUN
    runs = out_ref.shape[0] // 4
    sum_ref[...] = jnp.zeros_like(sum_ref)
    for a, b, c in OFFSETS:
        moved = mine + 4 * b + c
        away = pl.multiple_of(8 * (SPAN - 2 * a - (moved >> 3)), 8)
        place = 8 * place_of(a, b, c)
        sum_ref[pl.ds(away, 8), :] = sum_ref[pl.ds(away, 8), :] + recv_ref[moved & (RUN - 1), place : place + 8, :]
    parts = [sum_ref[pl.ds(k, 8, stride=8), :] for k in range(6)]
    lane = iota((8, 128), 1) // 16
    for quarter in range(4):
        for side in range(2):
            total = jnp.zeros((8, 128), F32)
            for k in range(6):
                turn = (16 * k - 64 * side - 16 * quarter) % 128
                piece = parts[k] if turn == 0 else pltpu.roll(parts[k], turn, axis=1)
                total = jnp.where(lane == k, piece, total)
            for o in range(2 * SPAN + 1):
                target = quarter * runs + ((run + o - SPAN) & (runs - 1))
                out_ref[target, :, 128 * side : 128 * side + 128] = total[o : o + 1]


def finish(recv_ref, mean_ref, force_ref, virial_ref):
    run = lax.axis_index("space") // RUN
    runs = recv_ref.shape[0] // 4
    totals = []
    for m in range(4):
        total = recv_ref[m * runs + run]
        for o in range(-SPAN, SPAN + 1):
            if o != 0:
                total = total + recv_ref[m * runs + ((run - o) & (runs - 1))]
        totals.append(total)
    mean = (totals[0] + totals[1] + totals[2] + totals[3]) * 0.25
    spread = jnp.zeros_like(mean)
    for total in totals:
        spread = spread + (total - mean) * (total - mean)
    spread = spread * 0.25

    def component(x, k):
        half = x[:, 128 * (k % 2) : 128 * (k % 2) + 128]
        turn = (-16 * (k // 2)) % 128
        return half if turn == 0 else pltpu.roll(half, turn, axis=1)

    for k in range(3):
        mean_ref[k, 0] = component(mean, k)[:, 0:16]
    force = component(spread, 0)
    for k in range(1, 3):
        force = force + component(spread, k)
    force_ref[0] = force[:, 0:16]
    virial = component(spread, 3)
    for k in range(4, 12):
        virial = virial + component(spread, k)
    virial_ref[0] = virial[:, 0:16]


def call(body, out_shape, scratch=(), limit=16 << 20, cost=None):
    return pl.pallas_call(
        body,
        out_shape=out_shape,
        scratch_shapes=list(scratch),
        compiler_params=pltpu.CompilerParams(vmem_limit_bytes=limit),
        cost_estimate=cost,
    )


def shaped(shape, dtype=F32):
    return jax.ShapeDtypeStruct(shape, dtype)


def local(
    positions, send_lists, neighbours,
    emb_scale, emb_shift, emb_middle, emb_mid_bias, emb_outer, emb_out_bias,
    fit_first, fit_first_bias, fit_second, fit_second_bias, fit_third, fit_third_bias, fit_readout,
):
    count = lax.axis_size("space")
    models = lax.axis_size("mp")
    runs = count // RUN
    packed = call(outgoing, shaped((count, 1, 384)))(send_lists, positions)
    arrived = lax.all_to_all(packed, "space", 0, 0)
    w2, w2t, w3, w3t, cols, ecols, f1, f1t, f2t, f3t = call(
        weights,
        (
            shaped((64, 32), BF16), shaped((32, 64), BF16), shaped((128, 64), BF16), shaped((64, 128), BF16),
            shaped((256, 128)), shaped((128, 128)), shaped((480, 896), BF16), shaped((896, 512), BF16),
            shaped((240, 240), BF16), shaped((240, 240), BF16),
        ),
        [pltpu.VMEM((128, 256), F32)],
    )(
        emb_scale, emb_shift, emb_middle, emb_mid_bias, emb_outer, emb_out_bias,
        fit_first, fit_first_bias, fit_second, fit_second_bias, fit_third, fit_third_bias, fit_readout,
    )
    pair = (ROWS, 128)
    terms = call(
        evaluate,
        shaped((RUN, 48, 128)),
        [
            pltpu.VMEM((12, 8, 128), I32), pltpu.VMEM((3, 8, 128), F32), pltpu.VMEM((8, 128), I32),
            pltpu.VMEM(pair, I32), pltpu.VMEM((3, *pair), F32), pltpu.VMEM(pair, F32), pltpu.VMEM((4, *pair), F32),
            pltpu.VMEM(pair, I32), pltpu.VMEM(pair, I32),
            pltpu.VMEM((ROWS, 32, 128), BF16), pltpu.VMEM((ROWS, 64, 128), BF16),
            pltpu.VMEM((ROWS, 128, 128), BF16), pltpu.VMEM((ROWS, 128, 128), BF16),
            pltpu.VMEM((4, 128, 128), F32), pltpu.VMEM((4, 112, 128), F32), pltpu.VMEM((4, 8, 128), F32),
            pltpu.VMEM((896, 128), BF16), pltpu.VMEM((896, 128), F32),
            pltpu.VMEM((4, 112, 128), F32), pltpu.VMEM((4, 128, 128), F32),
            pltpu.VMEM((4, *pair), F32), pltpu.VMEM(pair, F32), pltpu.VMEM((3, *pair), F32),
            pltpu.VMEM((224, 128), F32),
        ],
        32 << 20,
    )(arrived, neighbours, w2, w2t, w3, w3t, cols, ecols, f1, f1t, fit_second, f2t, fit_third, f3t)
    near = [[RUN * u + v for v in range(RUN)] for u in range(runs)]
    terms = lax.all_to_all(terms, "space", 0, 0, axis_index_groups=near)
    terms = call(regroup, shaped((models * runs, 1, 256)), [pltpu.VMEM((64, 128), F32)])(terms)
    far = [[m * count + RUN * u + v for m in range(models) for u in range(runs)] for v in range(RUN)]
    terms = lax.all_to_all(terms, ("mp", "space"), 0, 0, axis_index_groups=far)
    quarter = positions.shape[1] // models
    return call(
        finish, (shaped((3, 1, 1, quarter)), shaped((1, 1, quarter)), shaped((1, 1, quarter)))
    )(terms)


def solution(mesh):
    params = [P("mp", None)] * 2 + [P("mp", None, None), P("mp", None)] * 5 + [P("mp", None)]
    return jax.shard_map(
        local,
        mesh=mesh,
        in_specs=(P(None, "space"), P("space", None, None), P(None, "space"), *params),
        out_specs=(P(None, "space", "mp", None), P("space", "mp", None), P("space", "mp", None)),
        check_vma=False,
    )
```

time: 241 us -> 77.8 us (0.32)
  the two profiles are of different devices: /device:TPU:3 before, /device:TPU:1 now
where the time goes in v1:
time: 77.8 us; the launch traced here: 77.5 us
  blocking collectives  36.1 us (46%)
  Pallas kernels  15.6 us (20%)
  starting transfers between devices  14 us (18%)
  waiting for transfers between devices  8.24 us (11%)
  local copies, waits for them, and re-layouts  2.8 us (4%)
    all_to_all x1, blocking collectives, local(): terms = lax.all_to_all(terms, ('mp', 'space'), 0, 0, axis_index_groups=far)  27 us
    all_to_all x1, starting transfers between devices, local(): arrived = lax.all_to_all(packed, 'space', 0, 0)  14 us
    pallas_call x1, Pallas kernels, local(): call(evaluate, shaped((RUN, 48, 128)), [pltpu.VMEM((12, 8, 128), I32), pl...  12.6 us
    all_to_all x1, blocking collectives, local(): terms = lax.all_to_all(terms, 'space', 0, 0, axis_index_groups=near)  9.09 us
    all_to_all x1, waiting for transfers between devices, local(): arrived = lax.all_to_all(packed, 'space', 0, 0)  8.24 us
    unnamed x34, local copies, waits for them, and re-layouts  2.8 us
  transfers between devices with their start and end apart: 1, of which 1 were waited for; matrix products, arithmetic and copies ran while one was open for 0% of the time, Pallas kernels for 2%

profile of v1, /device:TPU:1, one launch (start us, length us, event | category | flops | bytes accessed | tf_op | source)
XLA Modules:
  0.0 77.5 jit_solution(12574557193062175521)
XLA Ops:
  0.6 0.0 copy-start.3
  0.6 0.7 copy.19.lists_ref
  1.3 0.0 copy-done.3
  1.3 0.8 shard_map.175
  2.1 0.0 copy-start.14
  2.1 0.0 copy-start.13
  2.1 0.0 copy-start.12
  2.1 0.0 copy-start.2
  2.1 14.0 %all-to-all-start = ((f32[128,1,384]{2,1,0:T(1,128)}), f32[128,1,384]{2,1,0:T(1,128)S(1)}, u32[]{:S(2)}, u32[]{:S(2)}) async-start(f32[128,1,384]{2,1,0:T(1,128)} %shard_map.175), calls=%async_computation | async-start | bytes 393216 | tf_op jit(solution)/shard_map/all_to_all | solution.py:482
  16.1 0.0 copy-done.14
  16.1 0.0 copy-start.1
  16.1 0.1 copy.20.mid_ref
  16.2 0.0 copy-done.13
  16.2 0.1 copy.21.outer_ref
  16.4 0.0 copy-done.12
  16.4 0.0 copy-start.4
  16.4 0.0 copy-start.5
  16.4 0.0 copy-start.6
  16.4 0.0 copy-start.7
  16.4 0.0 copy-start.8
  16.4 0.0 copy-start.9
  16.4 0.0 copy-start.10
  16.5 0.0 copy-start.11
  16.5 0.1 copy.22.nb_ref
  16.6 0.0 copy-done.2
  16.6 0.5 copy-done.1
  17.0 0.1 copy-done.4
  17.1 0.0 copy-done.5
  17.1 0.0 copy-done.6
  17.1 0.0 copy-done.7
  17.1 0.0 copy-done.8
  17.1 0.0 copy-done.9
  17.1 0.0 copy-done.10
  17.1 0.0 copy-done.11
  17.2 0.0 copy-start
  17.2 1.1 %copy-done = bf16[1,240,1600]{2,1,0:T(8,128)(2,1)S(1)} copy-done((bf16[1,240,1600]{2,1,0:T(8,128)(2,1)S(1)}, bf16[1,240,1600]{2,1,0:T(8,128)(2,1)}, u32[]{:S(2)}) %copy-start) | copy-done | bytes 768024
  18.3 1.3 %shard_map.176 = (bf16[64,32]{1,0:T(8,128)(2,1)S(1)}, bf16[32,64]{1,0:T(8,128)(2,1)S(1)}, bf16[128,64]{1,0:T(8,128)(2,1)S(1)}, bf16[64,128]{1,0:T(8,128)(2,1)S(1...) custom-call(f32[1,25]{1,0:T(1,128)S(1)} %copy-done.8, ...), custom_call_target="tpu_custom_call" | custom-call | tf_op jit(solution)/shard_map/pallas_call | solution.py:483
  19.6 8.2 %all-to-all-done.recv_ref = f32[128,1,384]{2,1,0:T(1,128)S(1)} async-done(((f32[128,1,384]{2,1,0:T(1,128)}), f32[128,1,384]{2,1,0:T(1,128)S(1)}, u32[]{:S(2)}, u32[]{:S(2)}) %all-to-all-start) | async-done | bytes 196640 | tf_op jit(solution)/shard_map/all_to_all | solution.py:482
  27.9 12.6 %shard_map.177 = f32[8,48,128]{2,1,0:T(8,128)S(1)} custom-call(f32[128,1,384]{2,1,0:T(1,128)S(1)} %all-to-all-done.recv_ref, s32[96,64]{1,0:T(8,128)S(1)} %copy.22.nb_ref, bf16[64,32]{1,0:T(8,128)(2,1)S(1)} %get-tuple-element.13.w2_ref, bf16[32,64]{1,0:T(8,128)(2,1)S(1)} %get-tuple-element.14.w2t_ref, bf16[128,64]{1,0:T(8,128)(2,1)S(1)} %get-tuple-element.15.w3_ref, ...), custom_call_target="tpu_custom_call" | custom-call | tf_op jit(solution)/shard_map/pallas_call | solution.py:496
  40.4 9.1 %all_to_all.15.recv_ref = f32[8,48,128]{2,1,0:T(8,128)S(1)} all-to-all(f32[8,48,128]{2,1,0:T(8,128)S(1)} %shard_map.177), channel_id=1, replica_groups={{0,1,2,3,4,5,6,7},{8,9,10,11,12,13,14,15},{16,17,18,19,20,21,22,23},{24..., dimensions={0} | all-to-all | bytes 393216 | tf_op jit(solution)/shard_map/all_to_all | solution.py:514
  49.5 0.3 shard_map.178
  49.8 27.0 %all_to_all.16.recv_ref = f32[64,1,256]{2,1,0:T(1,128)S(1)} all-to-all(f32[64,1,256]{2,1,0:T(1,128)S(1)} %shard_map.178), channel_id=1, replica_groups={{0,8,16,24,32,40,48,56,64,72,80,88,96,104,112,120,128,136,144,152,160,1..., dimensions={0} | all-to-all | bytes 131072 | tf_op jit(solution)/shard_map/all_to_all | solution.py:517
  76.8 0.7 shard_map.179
Async XLA Ops:
  0.6 0.7 copy-start.3
  2.1 14.0 %copy-start.14 = (bf16[1,50,25]{1,2,0:T(8,128)(2,1)S(1)}, bf16[1,50,25]{1,2,0:T(8,128)(2,1)}, u32[]{:S(2)}) copy-start(bf16[1,50,25]{1,2,0:T(8,128)(2,1)} %param.21) | copy-start | bytes 7504
  2.1 14.1 %copy-start.13 = (bf16[1,100,50]{1,2,0:T(8,128)(2,1)S(1)}, bf16[1,100,50]{1,2,0:T(8,128)(2,1)}, u32[]{:S(2)}) copy-start(bf16[1,100,50]{1,2,0:T(8,128)(2,1)} %param.23) | copy-start | bytes 30004
  2.1 14.3 %copy-start.12 = (s32[96,64]{0,1:T(8,128)S(1)}, s32[96,64]{0,1:T(8,128)}, u32[]{:S(2)}) copy-start(s32[96,64]{0,1:T(8,128)} %param.18) | copy-start | bytes 73732
  2.1 14.4 %copy-start.2 = (bf16[1,240,240]{2,1,0:T(8,128)(2,1)S(1)}, bf16[1,240,240]{2,1,0:T(8,128)(2,1)}, u32[]{:S(2)}) copy-start(bf16[1,240,240]{2,1,0:T(8,128)(2,1)} %f3_ref.1) | copy-start | bytes 345604
  2.1 25.7 %all-to-all-start = ((f32[128,1,384]{2,1,0:T(1,128)}), f32[128,1,384]{2,1,0:T(1,128)S(1)}, u32[]{:S(2)}, u32[]{:S(2)}) async-start(f32[128,1,384]{2,1,0:T(1,128)} %shard_map.175), calls=%async_computation | async-start | bytes 393216 | tf_op jit(solution)/shard_map/all_to_all | solution.py:482
  16.1 0.9 %copy-start.1 = (bf16[1,240,240]{2,1,0:T(8,128)(2,1)S(1)}, bf16[1,240,240]{2,1,0:T(8,128)(2,1)}, u32[]{:S(2)}) copy-start(bf16[1,240,240]{2,1,0:T(8,128)(2,1)} %f2_ref.1) | copy-start | bytes 345604
  16.4 0.7 copy-start.4
  16.4 0.7 copy-start.5
  16.4 0.7 copy-start.6
  16.4 0.7 copy-start.7
  16.4 0.7 copy-start.8
  16.4 0.7 copy-start.9
  16.4 0.7 copy-start.10
  16.5 0.7 copy-start.11
  17.2 1.1 %copy-start = (bf16[1,240,1600]{2,1,0:T(8,128)(2,1)S(1)}, bf16[1,240,1600]{2,1,0:T(8,128)(2,1)}, u32[]{:S(2)}) copy-start(bf16[1,240,1600]{2,1,0:T(8,128)(2,1)} %one_ref.1) | copy-start | bytes 2304004

commit v2 on v1

--- a/solution.py
+++ b/solution.py
@@ -50,10 +50,18 @@
     return lax.dot_general(a, b, (((1,), (1,)), ((), ())), preferred_element_type=F32)
 
 
-def outgoing(lists_ref, pos_ref, out_ref):
+def outgoing(lists_hbm, pos_hbm, out_ref, lists_ref, pos_ref, sems):
+    fetches = [
+        pltpu.make_async_copy(lists_hbm, lists_ref, sems.at[0]),
+        pltpu.make_async_copy(pos_hbm, pos_ref, sems.at[1]),
+    ]
+    for fetch in fetches:
+        fetch.start()
+    for fetch in fetches:
+        fetch.wait()
     count = out_ref.shape[0]
     me = lax.axis_index("space")
-    lists = lists_ref[0].astype(F32)
+    lists = lists_ref[:, 0, :].astype(F32)
     pos = pos_ref[...]
     row_xy = jnp.concatenate([pos[0:1], pos[1:2]], axis=1)
     row_z = jnp.concatenate([pos[2:3], pos[2:3]], axis=1)
@@ -85,8 +93,6 @@
 ):
     w2 = dot(dot(grouped(64, 50, True), mid_ref[0]).astype(BF16), grouped(25, 32, False)).astype(BF16)
     w3 = dot(dot(grouped(128, 100, True), outer_ref[0]).astype(BF16), grouped(50, 64, False)).astype(BF16)
-    w2_ref[...] = w2
-    w3_ref[...] = w3
     w2t_ref[...] = dot_last(eye(32), w2).astype(BF16)
     w3t_ref[...] = dot_last(eye(64), w3).astype(BF16)
     f2t_ref[...] = dot_last(eye(240), two_ref[0]).astype(BF16)
@@ -100,6 +106,11 @@
     ecols_ref[...] = jnp.zeros_like(ecols_ref)
     for q in range(4):
         ecols_ref[32 * q : 32 * q + 25, :] = turned[25 * q : 25 * q + 25]
+    for w, ref, column in ((w2, w2_ref, 2), (w3, w3_ref, 3)):
+        bias = jnp.broadcast_to(ecols_ref[0 : w.shape[0], column : column + 1], w.shape)
+        whole = bias.astype(BF16).astype(F32)
+        lane = iota(w.shape, 1)
+        ref[...] = jnp.where(lane == 25, whole, jnp.where(lane == 26, bias - whole, w.astype(F32))).astype(BF16)
     f1t_ref[...] = jnp.zeros_like(f1t_ref)
     for part in range(2):
         r, c = iota((256, 128), 0), iota((256, 128), 1)
@@ -185,7 +196,7 @@
     out_ref,
     num_ref, ext_ref, code_ref, idx_ref, off_ref, inv_ref, env_ref, hi_ref, lo_ref,
     s1_ref, s2_ref, s3_ref, h3_ref, mom_ref, nat_ref, axis_ref, feat_ref, dfeat_ref,
-    dnat_ref, dmom_ref, denv_ref, dinv_ref, grad_ref, acc_ref,
+    dnat_ref, denv_ref, dinv_ref, grad_ref, acc_ref,
 ):
     count = recv_ref.shape[0]
     me = lax.axis_index("space")
@@ -220,8 +231,8 @@
     mom_ref[...] = jnp.zeros_like(mom_ref)
     scale = jnp.broadcast_to(ecols_ref[0:32, 0:1], (32, 128))
     shift = jnp.broadcast_to(ecols_ref[0:32, 1:2], (32, 128))
-    bias_two = jnp.concatenate([jnp.broadcast_to(ecols_ref[0:64, 2:3], (64, 128))] * 8, axis=1)
-    bias_three = jnp.concatenate([jnp.broadcast_to(ecols_ref[0:128, 3:4], (128, 128))] * 8, axis=1)
+    constant = (iota((32, 128), 0) == 25) | (iota((32, 128), 0) == 26)
+    shift = jnp.where(constant, 40.0, shift)
 
     def forward(q, carry):
         base = pl.multiple_of(q * 8, 8)
@@ -231,10 +242,10 @@
             s1_ref[base + r] = (1.0 - t * t).astype(BF16)
             firsts.append(t.astype(BF16))
         h1 = jnp.concatenate(firsts, axis=1)
-        t2 = jnp.tanh(dot(w2_ref[...], h1) + bias_two)
+        t2 = jnp.tanh(dot(w2_ref[...], h1))
         h2 = (jnp.concatenate([h1, h1], axis=0).astype(F32) + t2).astype(BF16)
         s2 = (1.0 - t2 * t2).astype(BF16)
-        t3 = jnp.tanh(dot(w3_ref[...], h2) + bias_three)
+        t3 = jnp.tanh(dot(w3_ref[...], h2))
         h3 = (jnp.concatenate([h2, h2], axis=0).astype(F32) + t3).astype(BF16)
         s3 = (1.0 - t3 * t3).astype(BF16)
         for r in range(8):
@@ -242,17 +253,18 @@
             s2_ref[base + r] = s2[:, part]
             s3_ref[base + r] = s3[:, part]
             h3_ref[base + r] = h3[:, part]
+        env = [[env_ref[c, pl.ds(base + r, 1), :] for r in range(8)] for c in range(4)]
         for n in range(8):
             rows = slice(16 * n, 16 * n + 16)
             tiles = [h3[rows, 128 * r : 128 * r + 128].astype(F32) for r in range(8)]
             for c in range(4):
-                total = tiles[0] * env_ref[c, pl.ds(base, 1), :]
+                total = tiles[0] * env[c][0]
                 for r in range(1, 8):
-                    total = total + tiles[r] * env_ref[c, pl.ds(base + r, 1), :]
-                mom_ref[c, rows] = mom_ref[c, rows] + total
+                    total = total + tiles[r] * env[c][r]
+                mom_ref[c, rows] = mom_ref[c, rows] + total.astype(F32)
         return carry
 
-    lax.fori_loop(0, ROWS // 8, forward, 0)
+    lax.fori_loop(0, ROWS // 8, forward, 0, unroll=True)
 
     low = iota((1, 128), 1) < 64
     nat_ref[:, 96:112, :] = jnp.zeros((4, 16, 128), F32)
@@ -287,7 +299,7 @@
     split = jnp.concatenate([jnp.where(low, d1, 0.0), none, jnp.where(low, 0.0, d1), none], axis=0)
     dfeat_ref[...] = dot(f1t_ref[...], split.astype(BF16)).astype(BF16).astype(F32)
 
-    dmom_ref[...] = jnp.zeros_like(dmom_ref)
+    mom_ref[...] = jnp.zeros_like(mom_ref)
     for c in range(4):
         sums = [jnp.zeros((16, 128), F32)] * 8
         for blk in range(7):
@@ -303,38 +315,38 @@
         dnat_ref[c, 0:8] = dnat_ref[c, 0:8] + jnp.where(low, rows, turned)
         dnat_ref[c, 8:16] = dnat_ref[c, 8:16] + jnp.where(low, turned, rows)
         for q in range(4):
-            dmom_ref[c, 32 * q : 32 * q + 25] = dnat_ref[c, 25 * q : 25 * q + 25] * (1.0 / K)
+            mom_ref[c, 32 * q : 32 * q + 25] = dnat_ref[c, 25 * q : 25 * q + 25] * (1.0 / K)
 
     def backward(q, carry):
         base = pl.multiple_of(q * 8, 8)
         outer, pushed = [], []
         for r in range(8):
             env = [env_ref[c, pl.ds(base + r, 1), :] for c in range(4)]
-            parts = [jnp.zeros((16, 128), F32)] * 4
+            parts = [None] * 4
             tiles = []
             for n in range(8):
                 rows = slice(16 * n, 16 * n + 16)
-                dm = [dmom_ref[c, rows] for c in range(4)]
+                dm = [mom_ref[c, rows] for c in range(4)]
                 tiles.append((dm[0] * env[0] + dm[1] * env[1] + dm[2] * env[2] + dm[3] * env[3]).astype(BF16))
                 h = h3_ref[base + r, rows].astype(F32)
-                parts = [s + dm[c] * h for c, s in enumerate(parts)]
+                parts = [dm[c] * h if s is None else s + dm[c] * h for c, s in enumerate(parts)]
             for c in range(4):
                 denv_ref[c, pl.ds(base + r, 1), :] = jnp.sum(parts[c], axis=0, keepdims=True)
             d = jnp.concatenate(tiles, axis=0)
             outer.append(d)
-            pushed.append((d.astype(F32) * s3_ref[base + r].astype(F32)).astype(BF16))
+            pushed.append(d * s3_ref[base + r])
         d3 = jnp.concatenate(outer, axis=1)
-        back = dot(w3t_ref[...], jnp.concatenate(pushed, axis=1)).astype(BF16).astype(F32)
-        d2 = (back + d3[0:64].astype(F32) + d3[64:128].astype(F32)).astype(BF16)
+        back = dot(w3t_ref[...], jnp.concatenate(pushed, axis=1)).astype(BF16)
+        d2 = back + d3[0:64] + d3[64:128]
         s2 = jnp.concatenate([s2_ref[base + r] for r in range(8)], axis=1)
-        back = dot(w2t_ref[...], (d2.astype(F32) * s2.astype(F32)).astype(BF16)).astype(BF16).astype(F32)
-        d1 = (back + d2[0:32].astype(F32) + d2[32:64].astype(F32)).astype(BF16).astype(F32)
+        back = dot(w2t_ref[...], d2 * s2).astype(BF16)
+        d1 = (back + d2[0:32] + d2[32:64]).astype(F32)
         for r in range(8):
             d = d1[:, 128 * r : 128 * r + 128] * s1_ref[base + r].astype(F32) * scale
             dinv_ref[pl.ds(base + r, 1), :] = jnp.sum(d, axis=0, keepdims=True)
         return carry
 
-    lax.fori_loop(0, ROWS // 8, backward, 0)
+    lax.fori_loop(0, ROWS // 8, backward, 0, unroll=True)
 
     centre = [jnp.zeros((8, 128), F32)] * 3
     for q in range(ROWS // 8):
@@ -354,7 +366,7 @@
     acc_ref[...] = jnp.zeros_like(acc_ref)
     which = iota((8, 128), 0)
     lead, next_up, rest = which % 3 == 0, which % 3 == 1, which >= 6
-    spot = iota((128, 128), 0)
+    spot = iota((16, 128), 0).astype(F32).astype(BF16)
 
     def scatter(q, carry):
         base = pl.multiple_of(q * 8, 8)
@@ -369,13 +381,18 @@
             o_odd = jnp.where((which < 1) | rest, 1.0, jnp.where(which < 3, ox, jnp.where(which < 4, oy, oz)))
             halves = (-g_even * o_even, -g_odd * o_odd)
             term = jnp.concatenate([jnp.where(rest, t - t.astype(BF16).astype(F32), t) for t in halves], axis=0)
-            high = across(hi_ref[at, :], 16)
-            left.append(jnp.concatenate([jnp.where(high == h, term, 0.0).astype(BF16) for h in range(14)], axis=0))
-            right.append(jnp.where(spot == lo_ref[at, :], 1.0, 0.0).astype(BF16))
+            term = term.astype(BF16)
+            high = across(hi_ref[at, :], 16).astype(F32).astype(BF16)
+            place = across(lo_ref[at, :], 16).astype(F32).astype(BF16)
+            zero, one = jnp.zeros((16, 128), BF16), jnp.ones((16, 128), BF16)
+            left.append(jnp.concatenate([jnp.where(high == float(h), term, zero) for h in range(14)], axis=0))
+            right.append(
+                jnp.concatenate([jnp.where(spot + float(16 * n) == place, one, zero) for n in range(8)], axis=0)
+            )
         acc_ref[...] = acc_ref[...] + dot_last(jnp.concatenate(left, axis=1), jnp.concatenate(right, axis=1))
         return carry
 
-    lax.fori_loop(0, ROWS // 8, scatter, 0)
+    lax.fori_loop(0, ROWS // 8, scatter, 0, unroll=True)
 
     rows = [jnp.sum(s, axis=0, keepdims=True) for s in centre]
     rows = [s + half_turn(s) for s in rows]
@@ -456,13 +473,13 @@
     virial_ref[0] = virial[:, 0:16]
 
 
-def call(body, out_shape, scratch=(), limit=16 << 20, cost=None):
+def call(body, out_shape, scratch=(), limit=16 << 20, **specs):
     return pl.pallas_call(
         body,
         out_shape=out_shape,
         scratch_shapes=list(scratch),
         compiler_params=pltpu.CompilerParams(vmem_limit_bytes=limit),
-        cost_estimate=cost,
+        **specs,
     )
 
 
@@ -478,7 +495,16 @@
     count = lax.axis_size("space")
     models = lax.axis_size("mp")
     runs = count // RUN
-    packed = call(outgoing, shaped((count, 1, 384)))(send_lists, positions)
+    packed = call(
+        outgoing,
+        shaped((count, 1, 384)),
+        [
+            pltpu.VMEM((6, 1, 128), I32),
+            pltpu.VMEM(positions.shape, F32),
+            pltpu.SemaphoreType.DMA((2,)),
+        ],
+        in_specs=[pl.BlockSpec(memory_space=pltpu.HBM)] * 2,
+    )(jnp.transpose(send_lists, (1, 0, 2)), positions)
     arrived = lax.all_to_all(packed, "space", 0, 0)
     w2, w2t, w3, w3t, cols, ecols, f1, f1t, f2t, f3t = call(
         weights,
@@ -504,7 +530,7 @@
             pltpu.VMEM((ROWS, 128, 128), BF16), pltpu.VMEM((ROWS, 128, 128), BF16),
             pltpu.VMEM((4, 128, 128), F32), pltpu.VMEM((4, 112, 128), F32), pltpu.VMEM((4, 8, 128), F32),
             pltpu.VMEM((896, 128), BF16), pltpu.VMEM((896, 128), F32),
-            pltpu.VMEM((4, 112, 128), F32), pltpu.VMEM((4, 128, 128), F32),
+            pltpu.VMEM((4, 112, 128), F32),
             pltpu.VMEM((4, *pair), F32), pltpu.VMEM(pair, F32), pltpu.VMEM((3, *pair), F32),
             pltpu.VMEM((224, 128), F32),
         ],

time: 77.8 us -> 75.5 us (0.970)
  Pallas kernels: 15.6 us -> 12.5 us
    pallas_call x1, Pallas kernels: 12.6 us -> 9.46 us  [local(): call(evaluate, shaped((RUN, 48, 128)), [pltpu.VMEM((12, 8, 128), I32), pl...]
    unnamed x34 -> x35, local copies, waits for them, and re-layouts: 2.8 us -> 3.47 us
where the time goes in v2:
time: 75.5 us; the launch traced here: 75.1 us
  blocking collectives  36.1 us (48%)
  starting transfers between devices  14 us (19%)
  Pallas kernels  12.5 us (17%)
  waiting for transfers between devices  8.24 us (11%)
  local copies, waits for them, and re-layouts  3.47 us (5%)
  between operations  0.8 us (1%)
    all_to_all x1, blocking collectives, local(): terms = lax.all_to_all(terms, ('mp', 'space'), 0, 0, axis_index_groups=far)  27 us
    all_to_all x1, starting transfers between devices, local(): arrived = lax.all_to_all(packed, 'space', 0, 0)  14 us
    pallas_call x1, Pallas kernels, local(): call(evaluate, shaped((RUN, 48, 128)), [pltpu.VMEM((12, 8, 128), I32), pl...  9.46 us
    all_to_all x1, blocking collectives, local(): terms = lax.all_to_all(terms, 'space', 0, 0, axis_index_groups=near)  9.09 us
    all_to_all x1, waiting for transfers between devices, local(): arrived = lax.all_to_all(packed, 'space', 0, 0)  8.24 us
    unnamed x35, local copies, waits for them, and re-layouts  3.47 us
  transfers between devices with their start and end apart: 1, of which 1 were waited for; matrix products, arithmetic and copies ran while one was open for 0% of the time, Pallas kernels for 2%

profile of v2, /device:TPU:1, one launch (start us, length us, event | category | flops | bytes accessed | tf_op | source)
XLA Modules:
  0.0 75.1 jit_solution(14707778925374101384)
XLA Ops:
  0.6 0.0 copy-start.3
  0.6 0.7 copy-done.3
  1.3 0.0 copy-start.4
  1.3 0.7 copy-done.4
  2.0 0.8 %shard_map.175 = f32[128,1,384]{2,1,0:T(1,128)} custom-call(s32[6,1,128]{2,1,0:T(1,128)S(1)} %bitcast.1, f32[3,64]{1,0:T(4,128)S(1)} %copy-done.4), custom_call_target="tpu_custom_call" | custom-call | tf_op jit(solution)/shard_map/pallas_call | solution.py:498
  2.8 0.0 copy-start.15
  2.8 0.0 copy-start.14
  2.8 0.0 copy-start.13
  2.9 0.0 copy-start.2
  2.9 14.0 %all-to-all-start = ((f32[128,1,384]{2,1,0:T(1,128)}), f32[128,1,384]{2,1,0:T(1,128)S(1)}, u32[]{:S(2)}, u32[]{:S(2)}) async-start(f32[128,1,384]{2,1,0:T(1,128)} %shard_map.175), calls=%async_computation | async-start | bytes 393216 | tf_op jit(solution)/shard_map/all_to_all | solution.py:508
  16.9 0.0 copy-done.15
  16.9 0.0 copy-start.1
  16.9 0.1 copy.19.mid_ref
  17.0 0.0 copy-done.14
  17.0 0.1 copy.20.outer_ref
  17.1 0.0 copy-done.13
  17.1 0.0 copy-start.5
  17.1 0.0 copy-start.6
  17.1 0.0 copy-start.7
  17.2 0.0 copy-start.8
  17.2 0.0 copy-start.9
  17.2 0.0 copy-start.10
  17.2 0.0 copy-start.11
  17.2 0.0 copy-start.12
  17.2 0.1 copy.21.nb_ref
  17.3 0.0 copy-done.2
  17.3 0.5 copy-done.1
  17.8 0.1 copy-done.5
  17.8 0.0 copy-done.6
  17.8 0.0 copy-done.7
  17.9 0.0 copy-done.8
  17.9 0.0 copy-done.9
  17.9 0.0 copy-done.10
  17.9 0.0 copy-done.11
  17.9 0.0 copy-done.12
  17.9 0.0 copy-start
  17.9 1.1 %copy-done = bf16[1,240,1600]{2,1,0:T(8,128)(2,1)S(1)} copy-done((bf16[1,240,1600]{2,1,0:T(8,128)(2,1)S(1)}, bf16[1,240,1600]{2,1,0:T(8,128)(2,1)}, u32[]{:S(2)}) %copy-start) | copy-done | bytes 768024
  19.0 1.3 %shard_map.176 = (bf16[64,32]{1,0:T(8,128)(2,1)S(1)}, bf16[32,64]{1,0:T(8,128)(2,1)S(1)}, bf16[128,64]{1,0:T(8,128)(2,1)S(1)}, bf16[64,128]{1,0:T(8,128)(2,1)S(1...) custom-call(f32[1,25]{1,0:T(1,128)S(1)} %copy-done.9, ...), custom_call_target="tpu_custom_call" | custom-call | tf_op jit(solution)/shard_map/pallas_call | solution.py:509
  20.4 8.2 %all-to-all-done.recv_ref = f32[128,1,384]{2,1,0:T(1,128)S(1)} async-done(((f32[128,1,384]{2,1,0:T(1,128)}), f32[128,1,384]{2,1,0:T(1,128)S(1)}, u32[]{:S(2)}, u32[]{:S(2)}) %all-to-all-start) | async-done | bytes 196640 | tf_op jit(solution)/shard_map/all_to_all | solution.py:508
  28.6 9.5 %shard_map.177 = f32[8,48,128]{2,1,0:T(8,128)S(1)} custom-call(f32[128,1,384]{2,1,0:T(1,128)S(1)} %all-to-all-done.recv_ref, s32[96,64]{1,0:T(8,128)S(1)} %copy.21.nb_ref, bf16[64,32]{1,0:T(8,128)(2,1)S(1)} %get-tuple-element.13.w2_ref, bf16[32,64]{1,0:T(8,128)(2,1)S(1)} %get-tuple-element.14.w2t_ref, bf16[128,64]{1,0:T(8,128)(2,1)S(1)} %get-tuple-element.15.w3_ref, ...), custom_call_target="tpu_custom_call" | custom-call | tf_op jit(solution)/shard_map/pallas_call | solution.py:522
  38.1 9.1 %all_to_all.15.recv_ref = f32[8,48,128]{2,1,0:T(8,128)S(1)} all-to-all(f32[8,48,128]{2,1,0:T(8,128)S(1)} %shard_map.177), channel_id=1, replica_groups={{0,1,2,3,4,5,6,7},{8,9,10,11,12,13,14,15},{16,17,18,19,20,21,22,23},{24..., dimensions={0} | all-to-all | bytes 393216 | tf_op jit(solution)/shard_map/all_to_all | solution.py:540
  47.2 0.3 shard_map.178
  47.4 27.0 %all_to_all.16.recv_ref = f32[64,1,256]{2,1,0:T(1,128)S(1)} all-to-all(f32[64,1,256]{2,1,0:T(1,128)S(1)} %shard_map.178), channel_id=1, replica_groups={{0,8,16,24,32,40,48,56,64,72,80,88,96,104,112,120,128,136,144,152,160,1..., dimensions={0} | all-to-all | bytes 131072 | tf_op jit(solution)/shard_map/all_to_all | solution.py:543
  74.5 0.7 shard_map.179
Async XLA Ops:
  0.6 0.7 copy-start.3
  1.3 0.7 copy-start.4
  2.8 14.0 %copy-start.15 = (bf16[1,50,25]{1,2,0:T(8,128)(2,1)S(1)}, bf16[1,50,25]{1,2,0:T(8,128)(2,1)}, u32[]{:S(2)}) copy-start(bf16[1,50,25]{1,2,0:T(8,128)(2,1)} %param.21) | copy-start | bytes 7504
  2.8 14.2 %copy-start.14 = (bf16[1,100,50]{1,2,0:T(8,128)(2,1)S(1)}, bf16[1,100,50]{1,2,0:T(8,128)(2,1)}, u32[]{:S(2)}) copy-start(bf16[1,100,50]{1,2,0:T(8,128)(2,1)} %param.23) | copy-start | bytes 30004
  2.8 14.3 %copy-start.13 = (s32[96,64]{0,1:T(8,128)S(1)}, s32[96,64]{0,1:T(8,128)}, u32[]{:S(2)}) copy-start(s32[96,64]{0,1:T(8,128)} %param.18) | copy-start | bytes 73732
  2.9 14.5 %copy-start.2 = (bf16[1,240,240]{2,1,0:T(8,128)(2,1)S(1)}, bf16[1,240,240]{2,1,0:T(8,128)(2,1)}, u32[]{:S(2)}) copy-start(bf16[1,240,240]{2,1,0:T(8,128)(2,1)} %f3_ref.1) | copy-start | bytes 345604
  2.9 25.7 %all-to-all-start = ((f32[128,1,384]{2,1,0:T(1,128)}), f32[128,1,384]{2,1,0:T(1,128)S(1)}, u32[]{:S(2)}, u32[]{:S(2)}) async-start(f32[128,1,384]{2,1,0:T(1,128)} %shard_map.175), calls=%async_computation | async-start | bytes 393216 | tf_op jit(solution)/shard_map/all_to_all | solution.py:508
  16.9 0.9 %copy-start.1 = (bf16[1,240,240]{2,1,0:T(8,128)(2,1)S(1)}, bf16[1,240,240]{2,1,0:T(8,128)(2,1)}, u32[]{:S(2)}) copy-start(bf16[1,240,240]{2,1,0:T(8,128)(2,1)} %f2_ref.1) | copy-start | bytes 345604
  17.1 0.7 copy-start.5
  17.1 0.7 copy-start.6
  17.1 0.7 copy-start.7
  17.2 0.7 copy-start.8
  17.2 0.7 copy-start.9
  17.2 0.7 copy-start.10
  17.2 0.7 copy-start.11
  17.2 0.7 copy-start.12
  17.9 1.1 %copy-start = (bf16[1,240,1600]{2,1,0:T(8,128)(2,1)S(1)}, bf16[1,240,1600]{2,1,0:T(8,128)(2,1)}, u32[]{:S(2)}) copy-start(bf16[1,240,1600]{2,1,0:T(8,128)(2,1)} %one_ref.1) | copy-start | bytes 2304004

commit v3 on v2

--- a/solution.py
+++ b/solution.py
@@ -318,9 +318,9 @@
             mom_ref[c, 32 * q : 32 * q + 25] = dnat_ref[c, 25 * q : 25 * q + 25] * (1.0 / K)
 
     def backward(q, carry):
-        base = pl.multiple_of(q * 8, 8)
+        base = pl.multiple_of(q * 4, 4)
         outer, pushed = [], []
-        for r in range(8):
+        for r in range(4):
             env = [env_ref[c, pl.ds(base + r, 1), :] for c in range(4)]
             parts = [None] * 4
             tiles = []
@@ -338,15 +338,15 @@
         d3 = jnp.concatenate(outer, axis=1)
         back = dot(w3t_ref[...], jnp.concatenate(pushed, axis=1)).astype(BF16)
         d2 = back + d3[0:64] + d3[64:128]
-        s2 = jnp.concatenate([s2_ref[base + r] for r in range(8)], axis=1)
+        s2 = jnp.concatenate([s2_ref[base + r] for r in range(4)], axis=1)
         back = dot(w2t_ref[...], d2 * s2).astype(BF16)
         d1 = (back + d2[0:32] + d2[32:64]).astype(F32)
-        for r in range(8):
+        for r in range(4):
             d = d1[:, 128 * r : 128 * r + 128] * s1_ref[base + r].astype(F32) * scale
             dinv_ref[pl.ds(base + r, 1), :] = jnp.sum(d, axis=0, keepdims=True)
         return carry
 
-    lax.fori_loop(0, ROWS // 8, backward, 0, unroll=True)
+    lax.fori_loop(0, ROWS // 4, backward, 0, unroll=True)
 
     centre = [jnp.zeros((8, 128), F32)] * 3
     for q in range(ROWS // 8):
@@ -412,8 +412,8 @@
             tile = jnp.where(low, even_terms, half_turn(odd_terms))
         if (a, b, c) == (0, 0, 0):
             tile = tile + own
-        place = 8 * place_of(a, b, c)
-        out_ref[(mine - (4 * b + c)) & (RUN - 1), place : place + 8, :] = tile
+        place = 6 * place_of(a, b, c)
+        out_ref[(mine - (4 * b + c)) & (RUN - 1), place : place + 6, :] = tile[0:6]
 
 
 def regroup(recv_ref, out_ref, sum_ref):
@@ -424,8 +424,8 @@
     for a, b, c in OFFSETS:
         moved = mine + 4 * b + c
         away = pl.multiple_of(8 * (SPAN - 2 * a - (moved >> 3)), 8)
-        place = 8 * place_of(a, b, c)
-        sum_ref[pl.ds(away, 8), :] = sum_ref[pl.ds(away, 8), :] + recv_ref[moved & (RUN - 1), place : place + 8, :]
+        place = 6 * place_of(a, b, c)
+        sum_ref[pl.ds(away, 6), :] = sum_ref[pl.ds(away, 6), :] + recv_ref[moved & (RUN - 1), place : place + 6, :]
     parts = [sum_ref[pl.ds(k, 8, stride=8), :] for k in range(6)]
     lane = iota((8, 128), 1) // 16
     for quarter in range(4):
@@ -503,7 +503,8 @@
             pltpu.VMEM(positions.shape, F32),
             pltpu.SemaphoreType.DMA((2,)),
         ],
-        in_specs=[pl.BlockSpec(memory_space=pltpu.HBM)] * 2,
+        63 << 20,
+        in_specs=[pl.BlockSpec(memory_space=pl.ANY)] * 2,
     )(jnp.transpose(send_lists, (1, 0, 2)), positions)
     arrived = lax.all_to_all(packed, "space", 0, 0)
     w2, w2t, w3, w3t, cols, ecols, f1, f1t, f2t, f3t = call(
@@ -521,7 +522,7 @@
     pair = (ROWS, 128)
     terms = call(
         evaluate,
-        shaped((RUN, 48, 128)),
+        shaped((RUN, 36, 128)),
         [
             pltpu.VMEM((12, 8, 128), I32), pltpu.VMEM((3, 8, 128), F32), pltpu.VMEM((8, 128), I32),
             pltpu.VMEM(pair, I32), pltpu.VMEM((3, *pair), F32), pltpu.VMEM(pair, F32), pltpu.VMEM((4, *pair), F32),

time: 75.5 us -> 73.9 us (0.979)
  local copies, waits for them, and re-layouts: 3.47 us -> 2.11 us
    unnamed x35 -> x31, local copies, waits for them, and re-layouts: 3.47 us -> 2.11 us
where the time goes in v3:
time: 73.9 us; the launch traced here: 73.5 us
  blocking collectives  35.8 us (48%)
  starting transfers between devices  14 us (19%)
  Pallas kernels  12.6 us (17%)
  waiting for transfers between devices  8.24 us (11%)
  local copies, waits for them, and re-layouts  2.11 us (3%)
  between operations  0.79 us (1%)
    all_to_all x1, blocking collectives, local(): terms = lax.all_to_all(terms, ('mp', 'space'), 0, 0, axis_index_groups=far)  27 us
    all_to_all x1, starting transfers between devices, local(): arrived = lax.all_to_all(packed, 'space', 0, 0)  14 us
    pallas_call x1, Pallas kernels, local(): call(evaluate, shaped((RUN, 36, 128)), [pltpu.VMEM((12, 8, 128), I32), pl...  8.86 us
    all_to_all x1, blocking collectives, local(): terms = lax.all_to_all(terms, 'space', 0, 0, axis_index_groups=near)  8.78 us
    all_to_all x1, waiting for transfers between devices, local(): arrived = lax.all_to_all(packed, 'space', 0, 0)  8.24 us
    unnamed x31, local copies, waits for them, and re-layouts  2.11 us
    pallas_call x1, Pallas kernels, local(): call(outgoing, shaped((count, 1, 384)), [pltpu.VMEM((6, 1, 128), I32), pl...  1.49 us
  transfers between devices with their start and end apart: 1, of which 1 were waited for; matrix products, arithmetic and copies ran while one was open for 0% of the time, Pallas kernels for 2%

profile of v3, /device:TPU:1, one launch (start us, length us, event | category | flops | bytes accessed | tf_op | source)
XLA Modules:
  0.0 73.5 jit_solution(2938665844455778711)
XLA Ops:
  0.6 1.5 %shard_map.175 = f32[128,1,384]{2,1,0:T(1,128)} custom-call(s32[6,1,128]{2,1,0:T(1,128)} %bitcast.1, f32[3,64]{1,0:T(4,128)} %pos_hbm.1), custom_call_target="tpu_custom_call" | custom-call | tf_op jit(solution)/shard_map/pallas_call | solution.py:498
  2.1 0.0 copy-start.13
  2.1 0.0 copy-start.12
  2.2 0.0 copy-start.11
  2.2 0.0 copy-start.2
  2.2 14.0 %all-to-all-start = ((f32[128,1,384]{2,1,0:T(1,128)}), f32[128,1,384]{2,1,0:T(1,128)S(1)}, u32[]{:S(2)}, u32[]{:S(2)}) async-start(f32[128,1,384]{2,1,0:T(1,128)} %shard_map.175), calls=%async_computation | async-start | bytes 393216 | tf_op jit(solution)/shard_map/all_to_all | solution.py:509
  16.2 0.0 copy-done.13
  16.2 0.0 copy-start.1
  16.2 0.1 copy.19.mid_ref
  16.3 0.0 copy-done.12
  16.3 0.1 copy.20.outer_ref
  16.4 0.0 copy-done.11
  16.4 0.0 copy-start.3
  16.4 0.0 copy-start.4
  16.5 0.0 copy-start.5
  16.5 0.0 copy-start.6
  16.5 0.0 copy-start.7
  16.5 0.0 copy-start.8
  16.5 0.0 copy-start.9
  16.5 0.0 copy-start.10
  16.5 0.1 copy.21.nb_ref
  16.6 0.0 copy-done.2
  16.6 0.5 copy-done.1
  17.1 0.1 copy-done.3
  17.1 0.0 copy-done.4
  17.1 0.0 copy-done.5
  17.2 0.0 copy-done.6
  17.2 0.0 copy-done.7
  17.2 0.0 copy-done.8
  17.2 0.0 copy-done.9
  17.2 0.0 copy-done.10
  17.2 0.0 copy-start
  17.2 1.1 %copy-done = bf16[1,240,1600]{2,1,0:T(8,128)(2,1)S(1)} copy-done((bf16[1,240,1600]{2,1,0:T(8,128)(2,1)S(1)}, bf16[1,240,1600]{2,1,0:T(8,128)(2,1)}, u32[]{:S(2)}) %copy-start) | copy-done | bytes 768024
  18.4 1.3 %shard_map.176 = (bf16[64,32]{1,0:T(8,128)(2,1)S(1)}, bf16[32,64]{1,0:T(8,128)(2,1)S(1)}, bf16[128,64]{1,0:T(8,128)(2,1)S(1)}, bf16[64,128]{1,0:T(8,128)(2,1)S(1...) custom-call(f32[1,25]{1,0:T(1,128)S(1)} %copy-done.7, ...), custom_call_target="tpu_custom_call" | custom-call | tf_op jit(solution)/shard_map/pallas_call | solution.py:510
  19.7 8.2 %all-to-all-done.recv_ref = f32[128,1,384]{2,1,0:T(1,128)S(1)} async-done(((f32[128,1,384]{2,1,0:T(1,128)}), f32[128,1,384]{2,1,0:T(1,128)S(1)}, u32[]{:S(2)}, u32[]{:S(2)}) %all-to-all-start) | async-done | bytes 196640 | tf_op jit(solution)/shard_map/all_to_all | solution.py:509
  27.9 8.9 %shard_map.177 = f32[8,36,128]{2,1,0:T(8,128)S(1)} custom-call(f32[128,1,384]{2,1,0:T(1,128)S(1)} %all-to-all-done.recv_ref, s32[96,64]{1,0:T(8,128)S(1)} %copy.21.nb_ref, bf16[64,32]{1,0:T(8,128)(2,1)S(1)} %get-tuple-element.13.w2_ref, bf16[32,64]{1,0:T(8,128)(2,1)S(1)} %get-tuple-element.14.w2t_ref, bf16[128,64]{1,0:T(8,128)(2,1)S(1)} %get-tuple-element.15.w3_ref, ...), custom_call_target="tpu_custom_call" | custom-call | tf_op jit(solution)/shard_map/pallas_call | solution.py:523
  36.8 8.8 %all_to_all.15.recv_ref = f32[8,36,128]{2,1,0:T(8,128)S(1)} all-to-all(f32[8,36,128]{2,1,0:T(8,128)S(1)} %shard_map.177), channel_id=1, replica_groups={{0,1,2,3,4,5,6,7},{8,9,10,11,12,13,14,15},{16,17,18,19,20,21,22,23},{24..., dimensions={0} | all-to-all | bytes 294912 | tf_op jit(solution)/shard_map/all_to_all | solution.py:541
  45.6 0.3 shard_map.178
  45.8 27.0 %all_to_all.16.recv_ref = f32[64,1,256]{2,1,0:T(1,128)S(1)} all-to-all(f32[64,1,256]{2,1,0:T(1,128)S(1)} %shard_map.178), channel_id=1, replica_groups={{0,8,16,24,32,40,48,56,64,72,80,88,96,104,112,120,128,136,144,152,160,1..., dimensions={0} | all-to-all | bytes 131072 | tf_op jit(solution)/shard_map/all_to_all | solution.py:544
  72.9 0.7 shard_map.179
Async XLA Ops:
  2.1 14.0 %copy-start.13 = (bf16[1,50,25]{1,2,0:T(8,128)(2,1)S(1)}, bf16[1,50,25]{1,2,0:T(8,128)(2,1)}, u32[]{:S(2)}) copy-start(bf16[1,50,25]{1,2,0:T(8,128)(2,1)} %param.21) | copy-start | bytes 7504
  2.1 14.2 %copy-start.12 = (bf16[1,100,50]{1,2,0:T(8,128)(2,1)S(1)}, bf16[1,100,50]{1,2,0:T(8,128)(2,1)}, u32[]{:S(2)}) copy-start(bf16[1,100,50]{1,2,0:T(8,128)(2,1)} %param.23) | copy-start | bytes 30004
  2.2 14.3 %copy-start.11 = (s32[96,64]{0,1:T(8,128)S(1)}, s32[96,64]{0,1:T(8,128)}, u32[]{:S(2)}) copy-start(s32[96,64]{0,1:T(8,128)} %param.18) | copy-start | bytes 73732
  2.2 14.5 %copy-start.2 = (bf16[1,240,240]{2,1,0:T(8,128)(2,1)S(1)}, bf16[1,240,240]{2,1,0:T(8,128)(2,1)}, u32[]{:S(2)}) copy-start(bf16[1,240,240]{2,1,0:T(8,128)(2,1)} %f3_ref.1) | copy-start | bytes 345604
  2.2 25.7 %all-to-all-start = ((f32[128,1,384]{2,1,0:T(1,128)}), f32[128,1,384]{2,1,0:T(1,128)S(1)}, u32[]{:S(2)}, u32[]{:S(2)}) async-start(f32[128,1,384]{2,1,0:T(1,128)} %shard_map.175), calls=%async_computation | async-start | bytes 393216 | tf_op jit(solution)/shard_map/all_to_all | solution.py:509
  16.2 0.9 %copy-start.1 = (bf16[1,240,240]{2,1,0:T(8,128)(2,1)S(1)}, bf16[1,240,240]{2,1,0:T(8,128)(2,1)}, u32[]{:S(2)}) copy-start(bf16[1,240,240]{2,1,0:T(8,128)(2,1)} %f2_ref.1) | copy-start | bytes 345604
  16.4 0.7 copy-start.3
  16.4 0.7 copy-start.4
  16.5 0.7 copy-start.5
  16.5 0.7 copy-start.6
  16.5 0.7 copy-start.7
  16.5 0.7 copy-start.8
  16.5 0.7 copy-start.9
  16.5 0.7 copy-start.10
  17.2 1.1 %copy-start = (bf16[1,240,1600]{2,1,0:T(8,128)(2,1)S(1)}, bf16[1,240,1600]{2,1,0:T(8,128)(2,1)}, u32[]{:S(2)}) copy-start(bf16[1,240,1600]{2,1,0:T(8,128)(2,1)} %one_ref.1) | copy-start | bytes 2304004

commit v4 on v3

--- a/solution.py
+++ b/solution.py
@@ -64,14 +64,14 @@
     lists = lists_ref[:, 0, :].astype(F32)
     pos = pos_ref[...]
     row_xy = jnp.concatenate([pos[0:1], pos[1:2]], axis=1)
-    row_z = jnp.concatenate([pos[2:3], pos[2:3]], axis=1)
+    row_z = pos[2:3]
     for a, b, c in OFFSETS:
         target = lax.rem(me + step_of(a, b, c) + count, count)
         block = next((2 * s + (0 if v > 0 else 1) for s, v in enumerate((a, b, c)) if v), None)
         first = jnp.zeros((1, 128), F32) if block is None else lists[block : block + 1]
         out_ref[target, :, 0:128] = first
         out_ref[target, :, 128:256] = row_xy
-        out_ref[target, :, 256:384] = row_z
+        out_ref[target, :, 256:320] = row_z
 
 
 def grouped(rows, cols, by_row):
@@ -182,7 +182,8 @@
     for a, b, c in OFFSETS:
         e = source(a, b, c)
         row_xy = across(recv_ref[e, :, 128:256], 8)
-        row_z = across(recv_ref[e, :, 256:384], 8)
+        row_z = recv_ref[e, :, 256:320]
+        row_z = across(jnp.concatenate([row_z, row_z], axis=1), 8)
         here = owner == slot_of(a, b, c)
         got = (lanes_of(row_xy, atom), lanes_of(row_xy, atom + 64), lanes_of(row_z, atom))
         spots = [jnp.where(here, g - float(o), s) for g, o, s in zip(got, (a, b, c), spots)]
@@ -429,15 +430,17 @@
     parts = [sum_ref[pl.ds(k, 8, stride=8), :] for k in range(6)]
     lane = iota((8, 128), 1) // 16
     for quarter in range(4):
+        tiles = [jnp.zeros((8, 128), F32)] * 2
         for side in range(2):
-            total = jnp.zeros((8, 128), F32)
             for k in range(6):
-                turn = (16 * k - 64 * side - 16 * quarter) % 128
+                tile, group = divmod(6 * side + k, 8)
+                turn = (16 * (group - quarter) - 64 * side) % 128
                 piece = parts[k] if turn == 0 else pltpu.roll(parts[k], turn, axis=1)
-                total = jnp.where(lane == k, piece, total)
-            for o in range(2 * SPAN + 1):
-                target = quarter * runs + ((run + o - SPAN) & (runs - 1))
-                out_ref[target, :, 128 * side : 128 * side + 128] = total[o : o + 1]
+                tiles[tile] = jnp.where(lane == group, piece, tiles[tile])
+        for o in range(2 * SPAN + 1):
+            target = quarter * runs + ((run + o - SPAN) & (runs - 1))
+            out_ref[target, :, 0:128] = tiles[0][o : o + 1]
+            out_ref[target, :, 128:192] = tiles[1][o : o + 1, 0:64]
 
 
 def finish(recv_ref, mean_ref, force_ref, virial_ref):
@@ -457,20 +460,19 @@
     spread = spread * 0.25
 
     def component(x, k):
-        half = x[:, 128 * (k % 2) : 128 * (k % 2) + 128]
-        turn = (-16 * (k // 2)) % 128
-        return half if turn == 0 else pltpu.roll(half, turn, axis=1)
+        at = 16 * (6 * (k % 2) + k // 2)
+        return x[:, at : at + 16]
 
     for k in range(3):
-        mean_ref[k, 0] = component(mean, k)[:, 0:16]
+        mean_ref[k, 0] = component(mean, k)
     force = component(spread, 0)
     for k in range(1, 3):
         force = force + component(spread, k)
-    force_ref[0] = force[:, 0:16]
+    force_ref[0] = force
     virial = component(spread, 3)
     for k in range(4, 12):
         virial = virial + component(spread, k)
-    virial_ref[0] = virial[:, 0:16]
+    virial_ref[0] = virial
 
 
 def call(body, out_shape, scratch=(), limit=16 << 20, **specs):
@@ -497,7 +499,7 @@
     runs = count // RUN
     packed = call(
         outgoing,
-        shaped((count, 1, 384)),
+        shaped((count, 1, 320)),
         [
             pltpu.VMEM((6, 1, 128), I32),
             pltpu.VMEM(positions.shape, F32),
@@ -539,7 +541,7 @@
     )(arrived, neighbours, w2, w2t, w3, w3t, cols, ecols, f1, f1t, fit_second, f2t, fit_third, f3t)
     near = [[RUN * u + v for v in range(RUN)] for u in range(runs)]
     terms = lax.all_to_all(terms, "space", 0, 0, axis_index_groups=near)
-    terms = call(regroup, shaped((models * runs, 1, 256)), [pltpu.VMEM((64, 128), F32)])(terms)
+    terms = call(regroup, shaped((models * runs, 1, 192)), [pltpu.VMEM((64, 128), F32)])(terms)
     far = [[m * count + RUN * u + v for m in range(models) for u in range(runs)] for v in range(RUN)]
     terms = lax.all_to_all(terms, ("mp", "space"), 0, 0, axis_index_groups=far)
     quarter = positions.shape[1] // models

time: 73.9 us -> 73.9 us (level)
  no operation moved by 1% of the time
where the time goes in v4:
time: 73.9 us; the launch traced here: 73.5 us
  blocking collectives  35.8 us (48%)
  starting transfers between devices  14 us (19%)
  Pallas kernels  12.6 us (17%)
  waiting for transfers between devices  8.24 us (11%)
  local copies, waits for them, and re-layouts  2.11 us (3%)
  between operations  0.79 us (1%)
    all_to_all x1, blocking collectives, local(): terms = lax.all_to_all(terms, ('mp', 'space'), 0, 0, axis_index_groups=far)  27 us
    all_to_all x1, starting transfers between devices, local(): arrived = lax.all_to_all(packed, 'space', 0, 0)  14 us
    pallas_call x1, Pallas kernels, local(): call(evaluate, shaped((RUN, 36, 128)), [pltpu.VMEM((12, 8, 128), I32), pl...  8.85 us
    all_to_all x1, blocking collectives, local(): terms = lax.all_to_all(terms, 'space', 0, 0, axis_index_groups=near)  8.78 us
    all_to_all x1, waiting for transfers between devices, local(): arrived = lax.all_to_all(packed, 'space', 0, 0)  8.24 us
    unnamed x31, local copies, waits for them, and re-layouts  2.11 us
    pallas_call x1, Pallas kernels, local(): call(outgoing, shaped((count, 1, 320)), [pltpu.VMEM((6, 1, 128), I32), pl...  1.49 us
  transfers between devices with their start and end apart: 1, of which 1 were waited for; matrix products, arithmetic and copies ran while one was open for 0% of the time, Pallas kernels for 2%

profile of v4, /device:TPU:1, one launch (start us, length us, event | category | flops | bytes accessed | tf_op | source)
XLA Modules:
  0.0 73.5 jit_solution(10504094902595359053)
XLA Ops:
  0.6 1.5 %shard_map.175 = f32[128,1,320]{2,1,0:T(1,128)} custom-call(s32[6,1,128]{2,1,0:T(1,128)} %bitcast.1, f32[3,64]{1,0:T(4,128)} %pos_hbm.1), custom_call_target="tpu_custom_call" | custom-call | tf_op jit(solution)/shard_map/pallas_call | solution.py:500
  2.1 0.0 copy-start.13
  2.1 0.0 copy-start.12
  2.1 0.0 copy-start.11
  2.2 0.0 copy-start.2
  2.2 14.0 %all-to-all-start = ((f32[128,1,320]{2,1,0:T(1,128)}), f32[128,1,320]{2,1,0:T(1,128)S(1)}, u32[]{:S(2)}, u32[]{:S(2)}) async-start(f32[128,1,320]{2,1,0:T(1,128)} %shard_map.175), calls=%async_computation | async-start | bytes 393216 | tf_op jit(solution)/shard_map/all_to_all | solution.py:511
  16.2 0.0 copy-done.13
  16.2 0.0 copy-start.1
  16.2 0.1 copy.19.mid_ref
  16.3 0.0 copy-done.12
  16.3 0.1 copy.20.outer_ref
  16.4 0.0 copy-done.11
  16.4 0.0 copy-start.3
  16.4 0.0 copy-start.4
  16.5 0.0 copy-start.5
  16.5 0.0 copy-start.6
  16.5 0.0 copy-start.7
  16.5 0.0 copy-start.8
  16.5 0.0 copy-start.9
  16.5 0.0 copy-start.10
  16.5 0.1 copy.21.nb_ref
  16.6 0.0 copy-done.2
  16.6 0.5 copy-done.1
  17.1 0.1 copy-done.3
  17.1 0.0 copy-done.4
  17.1 0.0 copy-done.5
  17.2 0.0 copy-done.6
  17.2 0.0 copy-done.7
  17.2 0.0 copy-done.8
  17.2 0.0 copy-done.9
  17.2 0.0 copy-done.10
  17.2 0.0 copy-start
  17.2 1.1 %copy-done = bf16[1,240,1600]{2,1,0:T(8,128)(2,1)S(1)} copy-done((bf16[1,240,1600]{2,1,0:T(8,128)(2,1)S(1)}, bf16[1,240,1600]{2,1,0:T(8,128)(2,1)}, u32[]{:S(2)}) %copy-start) | copy-done | bytes 768024
  18.4 1.3 %shard_map.176 = (bf16[64,32]{1,0:T(8,128)(2,1)S(1)}, bf16[32,64]{1,0:T(8,128)(2,1)S(1)}, bf16[128,64]{1,0:T(8,128)(2,1)S(1)}, bf16[64,128]{1,0:T(8,128)(2,1)S(1...) custom-call(f32[1,25]{1,0:T(1,128)S(1)} %copy-done.7, ...), custom_call_target="tpu_custom_call" | custom-call | tf_op jit(solution)/shard_map/pallas_call | solution.py:512
  19.7 8.2 %all-to-all-done.recv_ref = f32[128,1,320]{2,1,0:T(1,128)S(1)} async-done(((f32[128,1,320]{2,1,0:T(1,128)}), f32[128,1,320]{2,1,0:T(1,128)S(1)}, u32[]{:S(2)}, u32[]{:S(2)}) %all-to-all-start) | async-done | bytes 163872 | tf_op jit(solution)/shard_map/all_to_all | solution.py:511
  27.9 8.9 %shard_map.177 = f32[8,36,128]{2,1,0:T(8,128)S(1)} custom-call(f32[128,1,320]{2,1,0:T(1,128)S(1)} %all-to-all-done.recv_ref, s32[96,64]{1,0:T(8,128)S(1)} %copy.21.nb_ref, bf16[64,32]{1,0:T(8,128)(2,1)S(1)} %get-tuple-element.13.w2_ref, bf16[32,64]{1,0:T(8,128)(2,1)S(1)} %get-tuple-element.14.w2t_ref, bf16[128,64]{1,0:T(8,128)(2,1)S(1)} %get-tuple-element.15.w3_ref, ...), custom_call_target="tpu_custom_call" | custom-call | tf_op jit(solution)/shard_map/pallas_call | solution.py:525
  36.8 8.8 %all_to_all.15.recv_ref = f32[8,36,128]{2,1,0:T(8,128)S(1)} all-to-all(f32[8,36,128]{2,1,0:T(8,128)S(1)} %shard_map.177), channel_id=1, replica_groups={{0,1,2,3,4,5,6,7},{8,9,10,11,12,13,14,15},{16,17,18,19,20,21,22,23},{24..., dimensions={0} | all-to-all | bytes 294912 | tf_op jit(solution)/shard_map/all_to_all | solution.py:543
  45.5 0.3 shard_map.178
  45.8 27.0 %all_to_all.16.recv_ref = f32[64,1,192]{2,1,0:T(1,128)S(1)} all-to-all(f32[64,1,192]{2,1,0:T(1,128)S(1)} %shard_map.178), channel_id=1, replica_groups={{0,8,16,24,32,40,48,56,64,72,80,88,96,104,112,120,128,136,144,152,160,1..., dimensions={0} | all-to-all | bytes 98304 | tf_op jit(solution)/shard_map/all_to_all | solution.py:546
  72.9 0.7 shard_map.179
Async XLA Ops:
  2.1 14.0 %copy-start.13 = (bf16[1,50,25]{1,2,0:T(8,128)(2,1)S(1)}, bf16[1,50,25]{1,2,0:T(8,128)(2,1)}, u32[]{:S(2)}) copy-start(bf16[1,50,25]{1,2,0:T(8,128)(2,1)} %param.21) | copy-start | bytes 7504
  2.1 14.2 %copy-start.12 = (bf16[1,100,50]{1,2,0:T(8,128)(2,1)S(1)}, bf16[1,100,50]{1,2,0:T(8,128)(2,1)}, u32[]{:S(2)}) copy-start(bf16[1,100,50]{1,2,0:T(8,128)(2,1)} %param.23) | copy-start | bytes 30004
  2.1 14.3 %copy-start.11 = (s32[96,64]{0,1:T(8,128)S(1)}, s32[96,64]{0,1:T(8,128)}, u32[]{:S(2)}) copy-start(s32[96,64]{0,1:T(8,128)} %param.18) | copy-start | bytes 73732
  2.2 14.5 %copy-start.2 = (bf16[1,240,240]{2,1,0:T(8,128)(2,1)S(1)}, bf16[1,240,240]{2,1,0:T(8,128)(2,1)}, u32[]{:S(2)}) copy-start(bf16[1,240,240]{2,1,0:T(8,128)(2,1)} %f3_ref.1) | copy-start | bytes 345604
  2.2 25.7 %all-to-all-start = ((f32[128,1,320]{2,1,0:T(1,128)}), f32[128,1,320]{2,1,0:T(1,128)S(1)}, u32[]{:S(2)}, u32[]{:S(2)}) async-start(f32[128,1,320]{2,1,0:T(1,128)} %shard_map.175), calls=%async_computation | async-start | bytes 393216 | tf_op jit(solution)/shard_map/all_to_all | solution.py:511
  16.2 0.9 %copy-start.1 = (bf16[1,240,240]{2,1,0:T(8,128)(2,1)S(1)}, bf16[1,240,240]{2,1,0:T(8,128)(2,1)}, u32[]{:S(2)}) copy-start(bf16[1,240,240]{2,1,0:T(8,128)(2,1)} %f2_ref.1) | copy-start | bytes 345604
  16.4 0.7 copy-start.3
  16.4 0.7 copy-start.4
  16.5 0.7 copy-start.5
  16.5 0.7 copy-start.6
  16.5 0.7 copy-start.7
  16.5 0.7 copy-start.8
  16.5 0.7 copy-start.9
  16.5 0.7 copy-start.10
  17.2 1.1 %copy-start = (bf16[1,240,1600]{2,1,0:T(8,128)(2,1)S(1)}, bf16[1,240,1600]{2,1,0:T(8,128)(2,1)}, u32[]{:S(2)}) copy-start(bf16[1,240,1600]{2,1,0:T(8,128)(2,1)} %one_ref.1) | copy-start | bytes 2304004

commit v5 on v4

--- a/solution.py
+++ b/solution.py
@@ -236,9 +236,9 @@
     shift = jnp.where(constant, 40.0, shift)
 
     def forward(q, carry):
-        base = pl.multiple_of(q * 8, 8)
+        base = pl.multiple_of(q * 12, 4)
         firsts = []
-        for r in range(8):
+        for r in range(12):
             t = jnp.tanh(scale * inv_ref[pl.ds(base + r, 1), :] + shift)
             s1_ref[base + r] = (1.0 - t * t).astype(BF16)
             firsts.append(t.astype(BF16))
@@ -249,23 +249,23 @@
         t3 = jnp.tanh(dot(w3_ref[...], h2))
         h3 = (jnp.concatenate([h2, h2], axis=0).astype(F32) + t3).astype(BF16)
         s3 = (1.0 - t3 * t3).astype(BF16)
-        for r in range(8):
+        for r in range(12):
             part = slice(128 * r, 128 * r + 128)
             s2_ref[base + r] = s2[:, part]
             s3_ref[base + r] = s3[:, part]
             h3_ref[base + r] = h3[:, part]
-        env = [[env_ref[c, pl.ds(base + r, 1), :] for r in range(8)] for c in range(4)]
+        env = [[env_ref[c, pl.ds(base + r, 1), :] for r in range(12)] for c in range(4)]
         for n in range(8):
             rows = slice(16 * n, 16 * n + 16)
-            tiles = [h3[rows, 128 * r : 128 * r + 128].astype(F32) for r in range(8)]
+            tiles = [h3[rows, 128 * r : 128 * r + 128].astype(F32) for r in range(12)]
             for c in range(4):
                 total = tiles[0] * env[c][0]
-                for r in range(1, 8):
+                for r in range(1, 12):
                     total = total + tiles[r] * env[c][r]
                 mom_ref[c, rows] = mom_ref[c, rows] + total.astype(F32)
         return carry
 
-    lax.fori_loop(0, ROWS // 8, forward, 0, unroll=True)
+    lax.fori_loop(0, ROWS // 12, forward, 0, unroll=True)
 
     low = iota((1, 128), 1) < 64
     nat_ref[:, 96:112, :] = jnp.zeros((4, 16, 128), F32)

time: 73.9 us -> 73.8 us (level)
  no operation moved by 1% of the time
where the time goes in v5:
time: 73.8 us; the launch traced here: 73.5 us
  blocking collectives  35.8 us (49%)
  starting transfers between devices  14 us (19%)
  Pallas kernels  12.6 us (17%)
  waiting for transfers between devices  8.24 us (11%)
  local copies, waits for them, and re-layouts  2.11 us (3%)
  between operations  0.79 us (1%)
    all_to_all x1, blocking collectives, local(): terms = lax.all_to_all(terms, ('mp', 'space'), 0, 0, axis_index_groups=far)  27 us
    all_to_all x1, starting transfers between devices, local(): arrived = lax.all_to_all(packed, 'space', 0, 0)  14 us
    pallas_call x1, Pallas kernels, local(): call(evaluate, shaped((RUN, 36, 128)), [pltpu.VMEM((12, 8, 128), I32), pl...  8.78 us
    all_to_all x1, blocking collectives, local(): terms = lax.all_to_all(terms, 'space', 0, 0, axis_index_groups=near)  8.78 us
    all_to_all x1, waiting for transfers between devices, local(): arrived = lax.all_to_all(packed, 'space', 0, 0)  8.24 us
    unnamed x31, local copies, waits for them, and re-layouts  2.11 us
    pallas_call x1, Pallas kernels, local(): call(outgoing, shaped((count, 1, 320)), [pltpu.VMEM((6, 1, 128), I32), pl...  1.49 us
  transfers between devices with their start and end apart: 1, of which 1 were waited for; matrix products, arithmetic and copies ran while one was open for 0% of the time, Pallas kernels for 2%

profile of v5, /device:TPU:1, one launch (start us, length us, event | category | flops | bytes accessed | tf_op | source)
XLA Modules:
  0.0 73.5 jit_solution(10292679246127188787)
XLA Ops:
  0.6 1.5 %shard_map.175 = f32[128,1,320]{2,1,0:T(1,128)} custom-call(s32[6,1,128]{2,1,0:T(1,128)} %bitcast.1, f32[3,64]{1,0:T(4,128)} %pos_hbm.1), custom_call_target="tpu_custom_call" | custom-call | tf_op jit(solution)/shard_map/pallas_call | solution.py:500
  2.1 0.0 copy-start.13
  2.1 0.0 copy-start.12
  2.1 0.0 copy-start.11
  2.2 0.0 copy-start.2
  2.2 14.0 %all-to-all-start = ((f32[128,1,320]{2,1,0:T(1,128)}), f32[128,1,320]{2,1,0:T(1,128)S(1)}, u32[]{:S(2)}, u32[]{:S(2)}) async-start(f32[128,1,320]{2,1,0:T(1,128)} %shard_map.175), calls=%async_computation | async-start | bytes 393216 | tf_op jit(solution)/shard_map/all_to_all | solution.py:511
  16.2 0.0 copy-done.13
  16.2 0.0 copy-start.1
  16.2 0.1 copy.19.mid_ref
  16.3 0.0 copy-done.12
  16.3 0.1 copy.20.outer_ref
  16.4 0.0 copy-done.11
  16.4 0.0 copy-start.3
  16.4 0.0 copy-start.4
  16.5 0.0 copy-start.5
  16.5 0.0 copy-start.6
  16.5 0.0 copy-start.7
  16.5 0.0 copy-start.8
  16.5 0.0 copy-start.9
  16.5 0.0 copy-start.10
  16.5 0.1 copy.21.nb_ref
  16.6 0.0 copy-done.2
  16.6 0.5 copy-done.1
  17.1 0.1 copy-done.3
  17.1 0.0 copy-done.4
  17.1 0.0 copy-done.5
  17.2 0.0 copy-done.6
  17.2 0.0 copy-done.7
  17.2 0.0 copy-done.8
  17.2 0.0 copy-done.9
  17.2 0.0 copy-done.10
  17.2 0.0 copy-start
  17.2 1.1 %copy-done = bf16[1,240,1600]{2,1,0:T(8,128)(2,1)S(1)} copy-done((bf16[1,240,1600]{2,1,0:T(8,128)(2,1)S(1)}, bf16[1,240,1600]{2,1,0:T(8,128)(2,1)}, u32[]{:S(2)}) %copy-start) | copy-done | bytes 768024
  18.4 1.3 %shard_map.176 = (bf16[64,32]{1,0:T(8,128)(2,1)S(1)}, bf16[32,64]{1,0:T(8,128)(2,1)S(1)}, bf16[128,64]{1,0:T(8,128)(2,1)S(1)}, bf16[64,128]{1,0:T(8,128)(2,1)S(1...) custom-call(f32[1,25]{1,0:T(1,128)S(1)} %copy-done.7, ...), custom_call_target="tpu_custom_call" | custom-call | tf_op jit(solution)/shard_map/pallas_call | solution.py:512
  19.7 8.2 %all-to-all-done.recv_ref = f32[128,1,320]{2,1,0:T(1,128)S(1)} async-done(((f32[128,1,320]{2,1,0:T(1,128)}), f32[128,1,320]{2,1,0:T(1,128)S(1)}, u32[]{:S(2)}, u32[]{:S(2)}) %all-to-all-start) | async-done | bytes 163872 | tf_op jit(solution)/shard_map/all_to_all | solution.py:511
  27.9 8.8 %shard_map.177 = f32[8,36,128]{2,1,0:T(8,128)S(1)} custom-call(f32[128,1,320]{2,1,0:T(1,128)S(1)} %all-to-all-done.recv_ref, s32[96,64]{1,0:T(8,128)S(1)} %copy.21.nb_ref, bf16[64,32]{1,0:T(8,128)(2,1)S(1)} %get-tuple-element.13.w2_ref, bf16[32,64]{1,0:T(8,128)(2,1)S(1)} %get-tuple-element.14.w2t_ref, bf16[128,64]{1,0:T(8,128)(2,1)S(1)} %get-tuple-element.15.w3_ref, ...), custom_call_target="tpu_custom_call" | custom-call | tf_op jit(solution)/shard_map/pallas_call | solution.py:525
  36.7 8.8 %all_to_all.15.recv_ref = f32[8,36,128]{2,1,0:T(8,128)S(1)} all-to-all(f32[8,36,128]{2,1,0:T(8,128)S(1)} %shard_map.177), channel_id=1, replica_groups={{0,1,2,3,4,5,6,7},{8,9,10,11,12,13,14,15},{16,17,18,19,20,21,22,23},{24..., dimensions={0} | all-to-all | bytes 294912 | tf_op jit(solution)/shard_map/all_to_all | solution.py:543
  45.5 0.3 shard_map.178
  45.8 27.0 %all_to_all.16.recv_ref = f32[64,1,192]{2,1,0:T(1,128)S(1)} all-to-all(f32[64,1,192]{2,1,0:T(1,128)S(1)} %shard_map.178), channel_id=1, replica_groups={{0,8,16,24,32,40,48,56,64,72,80,88,96,104,112,120,128,136,144,152,160,1..., dimensions={0} | all-to-all | bytes 98304 | tf_op jit(solution)/shard_map/all_to_all | solution.py:546
  72.8 0.7 shard_map.179
Async XLA Ops:
  2.1 14.0 %copy-start.13 = (bf16[1,50,25]{1,2,0:T(8,128)(2,1)S(1)}, bf16[1,50,25]{1,2,0:T(8,128)(2,1)}, u32[]{:S(2)}) copy-start(bf16[1,50,25]{1,2,0:T(8,128)(2,1)} %param.21) | copy-start | bytes 7504
  2.1 14.2 %copy-start.12 = (bf16[1,100,50]{1,2,0:T(8,128)(2,1)S(1)}, bf16[1,100,50]{1,2,0:T(8,128)(2,1)}, u32[]{:S(2)}) copy-start(bf16[1,100,50]{1,2,0:T(8,128)(2,1)} %param.23) | copy-start | bytes 30004
  2.1 14.3 %copy-start.11 = (s32[96,64]{0,1:T(8,128)S(1)}, s32[96,64]{0,1:T(8,128)}, u32[]{:S(2)}) copy-start(s32[96,64]{0,1:T(8,128)} %param.18) | copy-start | bytes 73732
  2.2 14.5 %copy-start.2 = (bf16[1,240,240]{2,1,0:T(8,128)(2,1)S(1)}, bf16[1,240,240]{2,1,0:T(8,128)(2,1)}, u32[]{:S(2)}) copy-start(bf16[1,240,240]{2,1,0:T(8,128)(2,1)} %f3_ref.1) | copy-start | bytes 345604
  2.2 25.7 %all-to-all-start = ((f32[128,1,320]{2,1,0:T(1,128)}), f32[128,1,320]{2,1,0:T(1,128)S(1)}, u32[]{:S(2)}, u32[]{:S(2)}) async-start(f32[128,1,320]{2,1,0:T(1,128)} %shard_map.175), calls=%async_computation | async-start | bytes 393216 | tf_op jit(solution)/shard_map/all_to_all | solution.py:511
  16.2 0.9 %copy-start.1 = (bf16[1,240,240]{2,1,0:T(8,128)(2,1)S(1)}, bf16[1,240,240]{2,1,0:T(8,128)(2,1)}, u32[]{:S(2)}) copy-start(bf16[1,240,240]{2,1,0:T(8,128)(2,1)} %f2_ref.1) | copy-start | bytes 345604
  16.4 0.7 copy-start.3
  16.4 0.7 copy-start.4
  16.5 0.7 copy-start.5
  16.5 0.7 copy-start.6
  16.5 0.7 copy-start.7
  16.5 0.7 copy-start.8
  16.5 0.7 copy-start.9
  16.5 0.7 copy-start.10
  17.2 1.1 %copy-start = (bf16[1,240,1600]{2,1,0:T(8,128)(2,1)S(1)}, bf16[1,240,1600]{2,1,0:T(8,128)(2,1)}, u32[]{:S(2)}) copy-start(bf16[1,240,1600]{2,1,0:T(8,128)(2,1)} %one_ref.1) | copy-start | bytes 2304004
